TPU v7x, 128 devices: a whole 4x4x4 slice. The times are simulated.
128 devices in a mesh: dom: 16 (over x, y), grp: 8 (over z, core).
Axes of the slice: x: 4, y: 4, z: 4, core: 2. Of those that a mesh axis runs over, the one named last changes fastest.
Arguments:
- solved: bfloat16 [16, 8192, 512], P('dom', 'grp'), may hold values from -6 to 6
- e_blocks: bfloat16 [16, 6, 8192, 1024], P('dom', None, 'grp'), may hold values from -0.09375 to 0.09375
- block_mask: int32 [16, 6, 8], P('dom', None, 'grp'), may hold values 0 or 1
- owner: int32 [16, 6, 1], P('dom'), may hold values from 0 to 15; in each aligned block of 6 rows (0 to 5, 6 to 11, ..., all dimensions but the last counted through in order) at most 2 rows name the same one
- local_id: int32 [16, 6], P('dom'), may hold values from 0 to 3
Outputs:
- schur: bfloat16 [64, 1024, 512], P('dom', 'grp')
Inputs may be any that keep to these rules, and one draw needn't show every extreme that they name: Among the 6 slots of one subdomain at most 2 have the same owner, and in some subdomain exactly 2 do.
All inputs are finite; a program needn't handle non-finite values. No bound on the sum of `block_mask` on one device may be relied on, other than what follows from the above.
Results may differ from a plain program's by a relative error of at most 0.015.
Values may be sent and summed in bfloat16 or wider, within the bound.
No kernel may reach another device: no remote copies, remote signals or barrier semaphores. Data moves between devices by JAX's collectives and lax.ppermute only.
A program may use at most 128 MiB of HBM per device.

v0:
```python
import jax
import jax.numpy as jnp
from jax import lax
from jax.sharding import PartitionSpec as P

BLK = 1024
COLS = 512
SLOTS = 6
OWN = 4
CAP = 2


def on_device(solved, e_blocks, block_mask, owner, local_id):
    present = block_mask[0].astype(jnp.float32)
    block_rows = BLK // lax.axis_size("grp")
    coupling = e_blocks[0, :, 0:BLK, :]
    factor = solved[0, 0:BLK, :]
    product = jnp.einsum("sjk,jc->ksc", coupling, factor, preferred_element_type=jnp.float32)
    total = product * present[:, 0][None, :, None]
    rounded = lax.optimization_barrier(total.reshape(BLK, SLOTS * COLS).astype(jnp.bfloat16))
    summed = lax.psum_scatter(
        rounded.astype(jnp.float32).astype(jnp.bfloat16), "grp", scatter_dimension=0, tiled=True
    )
    pieces = summed.reshape(block_rows, SLOTS, COLS)
    owned_ids = jnp.arange(OWN, dtype=jnp.int32)
    domains = lax.axis_size("dom")
    targets = owner[0, :, 0]
    slot_ids = jnp.arange(SLOTS, dtype=jnp.int32)
    earlier = (targets[:, None] == targets[None, :]) & (slot_ids[None, :] < slot_ids[:, None])
    position = jnp.sum(earlier.astype(jnp.int32), axis=1)
    domain_ids = jnp.arange(domains, dtype=jnp.int32)
    capacity_ids = jnp.arange(CAP, dtype=jnp.int32)
    placing = (targets[None, None, :] == domain_ids[:, None, None]) & (
        position[None, None, :] == capacity_ids[None, :, None]
    )
    placing = placing.reshape(domains * CAP, SLOTS)
    outgoing = jnp.einsum(
        "rsc,ts->rtc", pieces, placing.astype(jnp.bfloat16), preferred_element_type=jnp.float32
    ).astype(jnp.bfloat16)
    labels = jnp.sum(placing.astype(jnp.int32) * (local_id[0] + 1)[None, :], axis=1)[None, :]
    incoming, arrived = (
        lax.all_to_all(outgoing, "dom", split_axis=1, concat_axis=1, tiled=True),
        lax.all_to_all(labels, "dom", split_axis=1, concat_axis=1, tiled=True),
    )
    select = arrived[0][:, None] - 1 == owned_ids[None, :]
    result = jnp.einsum(
        "rtc,to->orc", incoming, select.astype(jnp.bfloat16), preferred_element_type=jnp.float32
    )
    return result.astype(jnp.bfloat16)


def solution(mesh):
    in_specs = (
        P("dom", "grp", None),
        P("dom", None, "grp", None),
        P("dom", None, "grp"),
        P("dom", None, None),
        P("dom", None),
    )
    out_specs = P("dom", "grp", None)
    return jax.shard_map(
        on_device, mesh=mesh, in_specs=in_specs, out_specs=out_specs, check_vma=False
    )
```

profile of v0, /device:TPU:53, one launch (start us, length us, event | category | flops | bytes accessed | tf_op | source)
XLA Modules:
  0.0 164.4 jit_solution(12946360419070291153)
XLA Ops:
  6.5 0.0 copy-start
  6.5 0.0 reduce-scatter.4.cloned.1.call-start
  6.5 0.7 convert_bitcast_fusion.1
  7.3 0.5 copy-done
  7.8 13.2 %multiply_convert_fusion = bf16[512,6,1024]{2,0,1:T(8,128)(2,1)} fusion(f32[6]{0:T(128)S(1)} %convert_bitcast_fusion.1, bf16[1,6,1024,1024]{3,2,1,0:T(8,128)(2,1)} %param.6, bf16[1,1024,512]{2,1,0:T(8,128)(2,1)S(1)} %copy-done), kind=kOutput, calls=%fused_computation.2 | convolution fusion | flops 6448742400 | bytes 19922968 | tf_op jit(solution)/shard_map/sjk,jc->ksc/dot_general | solution.py:18
  21.0 8.7 %copy.34 = bf16[1024,3072]{1,0:T(8,128)(2,1)} copy(bf16[1024,3072]{0,1:T(8,128)(2,1)} %bitcast.32) | data formatting | bytes 12582912
  29.7 0.0 copy-start.1
  29.7 0.0 copy-start.2
  29.7 0.0 reduce-scatter.4.cloned.1.call-update
  29.7 0.6 copy-done.1
  30.3 0.2 convert_reduce_fusion
  30.5 0.0 copy-done.2
  30.6 1.0 select_reduce_fusion
  31.5 6.7 %all-to-all-start = ((s32[1,16,2]{2,0,1:T(1,128)}), s32[1,16,2]{2,0,1:T(1,128)S(1)}, u32[]{:S(2)}, u32[]{:S(2)}) async-start(s32[1,16,2]{2,0,1:T(1,128)} %bitcast.14), calls=%async_computation | async-start | bytes 16384 | tf_op jit(solution)/shard_map/all_to_all | solution.py:43
  38.2 35.1 %reduce-scatter.4.cloned.1.call-done = bf16[128,3072]{1,0:T(8,128)(2,1)} async-done(((bf16[1024,3072]{1,0:T(8,128)(2,1)}), bf16[128,3072]{1,0:T(8,128)(2,1)}) %reduce-scatter.4.cloned.1.call-update) | async-done | bytes 786448
  73.3 1.6 copy.35
  74.9 0.9 copy.24
  75.8 1.2 convert_bitcast_fusion
  77.0 4.4 %copy.25 = bf16[128,32,512]{2,0,1:T(8,128)(2,1)} copy(bf16[128,32,512]{2,1,0:T(8,128)(2,1)S(1)} %convert_bitcast_fusion) | data formatting | bytes 8388608 | tf_op jit(solution)/shard_map/convert_element_type | solution.py:39
  81.4 0.0 all-to-all-done
  81.4 6.7 %all-to-all-start.1 = ((bf16[128,32,512]{2,0,1:T(8,128)(2,1)}), bf16[128,32,512]{2,0,1:T(8,128)(2,1)}, u32[]{:S(2)}, u32[]{:S(2)}) async-start(bf16[128,32,512]{2,0,1:T(8,128)(2,1)} %copy.25), calls=%async_computation.1 | async-start | bytes 8388608 | tf_op jit(solution)/shard_map/all_to_all | solution.py:42
  88.1 0.1 sub.7
  88.2 63.8 %all-to-all-done.1 = bf16[128,32,512]{2,0,1:T(8,128)(2,1)} async-done(((bf16[128,32,512]{2,0,1:T(8,128)(2,1)}), bf16[128,32,512]{2,0,1:T(8,128)(2,1)}, u32[]{:S(2)}, u32[]{:S(2)}) %all-to-all-start.1) | async-done | bytes 4194336 | tf_op jit(solution)/shard_map/all_to_all | solution.py:42
  152.0 4.6 %fusion.6 = bf16[4,128,512]{2,0,1:T(4,128)(2,1)S(1)} fusion(bf16[128,32,512]{2,0,1:T(8,128)(2,1)} %all-to-all-done.1, s32[32]{0:T(128)S(1)} %sub.7), kind=kOutput, calls=%fused_computation.6 | convolution fusion | flops 17039488 | bytes 4718720 | tf_op jit(solution)/shard_map/rtc,to->orc/dot_general | solution.py:46
  156.6 0.9 copy.27
  (5 shorter events, 0.1 us)
Async XLA Ops:
  6.5 1.2 copy-start
  6.5 66.8 %reduce-scatter.4.cloned.1.call-start = ((), (), s32[]{:S(2)}) async-start(), calls=%async_computation.3 | async-start | bytes 7077888
  29.7 0.7 copy-start.1
  29.7 0.8 copy-start.2
  31.5 49.9 %all-to-all-start = ((s32[1,16,2]{2,0,1:T(1,128)}), s32[1,16,2]{2,0,1:T(1,128)S(1)}, u32[]{:S(2)}, u32[]{:S(2)}) async-start(s32[1,16,2]{2,0,1:T(1,128)} %bitcast.14), calls=%async_computation | async-start | bytes 16384 | tf_op jit(solution)/shard_map/all_to_all | solution.py:43
  81.4 70.6 %all-to-all-start.1 = ((bf16[128,32,512]{2,0,1:T(8,128)(2,1)}), bf16[128,32,512]{2,0,1:T(8,128)(2,1)}, u32[]{:S(2)}, u32[]{:S(2)}) async-start(bf16[128,32,512]{2,0,1:T(8,128)(2,1)} %copy.25), calls=%async_computation.1 | async-start | bytes 8388608 | tf_op jit(solution)/shard_map/all_to_all | solution.py:42
Sparse Core Ops, SparseCore 0:
  29.8 43.4 reduce-scatter.3
where the time goes:
time: 165 us; the launch traced here: 164 us
  waiting for transfers between devices  99 us (60%)
  matrix products  19.1 us (12%)
  local copies, waits for them, and re-layouts  17.6 us (11%)
  between operations  13.4 us (8%)
  starting transfers between devices  13.3 us (8%)
  other arithmetic  1.92 us (1%)
    all_to_all x1, waiting for transfers between devices, on_device(): lax.all_to_all(outgoing, 'dom', split_axis=1, concat_axis=1, tiled=True)  63.8 us
    unnamed x2, waiting for transfers between devices  35.1 us
    dot_general x1, matrix products, on_device(): jnp.einsum('sjk,jc->ksc', coupling, factor, preferred_element_type=jnp.fl...  13.2 us
    unnamed x8, local copies, waits for them, and re-layouts  11.4 us
    all_to_all x1, starting transfers between devices, on_device(): lax.all_to_all(outgoing, 'dom', split_axis=1, concat_axis=1, tiled=True)  6.67 us
    all_to_all x1, starting transfers between devices, on_device(): lax.all_to_all(labels, 'dom', split_axis=1, concat_axis=1, tiled=True)  6.67 us
    dot_general x1, matrix products, on_device(): jnp.einsum('rtc,to->orc', incoming, select.astype(jnp.bfloat16), preferre...  4.63 us
    convert_element_type x1, local copies, waits for them, and re-layouts, on_device(): outgoing = jnp.einsum('rsc,ts->rtc', pieces, placing.astype(jnp.bfloat16)...  4.37 us
  transfers between devices with their start and end apart: 3, of which 2 were waited for; matrix products, arithmetic and copies ran while one was open for 6% of the time, Pallas kernels for 0%

commit v1 on v0

v1 whole, which is shorter than its diff:
```python
import functools
import jax
import jax.numpy as jnp
from jax import lax
from jax.experimental import pallas as pl
from jax.experimental.pallas import tpu as pltpu
from jax.sharding import PartitionSpec as P

BLK = 1024
COLS = 512
SLOTS = 6
OWN = 4
N_DOM = 16
N_GRP = 8
N_Z = 4
LANES = BLK // N_GRP
PIECE = COLS // N_DOM
CHUNKS = ((0, 3), (3, 3))


def product_kernel(first, mask_ref, factor_ref, coupling_ref, own0, own1, own2, own3, other, turned):
    group = lax.axis_index("grp")
    plane = lax.div(group, 2)
    core = lax.rem(group, 2)
    slot = pl.program_id(0)

    @pl.when(slot == 0)
    def _():
        turned[...] = factor_ref[0].T

    present = mask_ref[first + slot].astype(jnp.float32)
    for k, own in enumerate((own0, own1, own2, own3)):
        start = pl.multiple_of(lax.rem(plane + k, N_Z) * (2 * LANES), 2 * LANES)
        both = jnp.dot(
            turned[...],
            coupling_ref[:, pl.ds(start, 2 * LANES)],
            preferred_element_type=jnp.float32,
        )
        both = both * present
        low, high = both[:, :LANES], both[:, LANES:]
        mine = jnp.where(core == 0, low, high).astype(jnp.bfloat16)
        theirs = jnp.where(core == 0, high, low).astype(jnp.bfloat16)
        own[...] = mine.reshape(N_DOM, PIECE, LANES)
        other[k] = theirs.reshape(N_DOM, PIECE, LANES)


def product(solved, e_blocks, mask, first, count):
    shape = (N_DOM, count, PIECE, LANES)
    block = (N_DOM, None, PIECE, LANES)
    return pl.pallas_call(
        functools.partial(product_kernel, first),
        grid=(count,),
        in_specs=[
            pl.BlockSpec(memory_space=pltpu.SMEM),
            pl.BlockSpec((1, BLK, COLS), lambda s: (0, 0, 0)),
            pl.BlockSpec((None, None, BLK, BLK), lambda s: (0, first + s, 0, 0)),
        ],
        out_specs=[pl.BlockSpec(block, lambda s: (0, s, 0, 0))] * N_Z
        + [pl.BlockSpec((N_Z,) + block, lambda s: (0, 0, s, 0, 0))],
        out_shape=[jax.ShapeDtypeStruct(shape, jnp.bfloat16)] * N_Z
        + [jax.ShapeDtypeStruct((N_Z,) + shape, jnp.bfloat16)],
        scratch_shapes=[pltpu.VMEM((COLS, BLK), jnp.bfloat16)],
        compiler_params=pltpu.CompilerParams(vmem_limit_bytes=40 << 20),
        name="product",
    )(mask, solved, e_blocks)


def gather_kernel(target_ref, items_ref, out_ref, total):
    total[...] = jnp.zeros_like(total)

    def add(i, _):
        for s in range(SLOTS):
            t = target_ref[i * SLOTS + s]
            total[t] = total[t] + items_ref[i, s].astype(jnp.float32)
        return 0

    lax.fori_loop(0, N_DOM, add, 0)
    out_ref[...] = total[...].astype(jnp.bfloat16)


def sum_blocks(target, items):
    return pl.pallas_call(
        gather_kernel,
        in_specs=[
            pl.BlockSpec(memory_space=pltpu.SMEM),
            pl.BlockSpec(memory_space=pltpu.VMEM),
        ],
        out_specs=pl.BlockSpec(memory_space=pltpu.VMEM),
        out_shape=jax.ShapeDtypeStruct((N_DOM * OWN, PIECE, LANES), jnp.bfloat16),
        scratch_shapes=[pltpu.VMEM((N_DOM * OWN, PIECE, LANES), jnp.float32)],
        compiler_params=pltpu.CompilerParams(vmem_limit_bytes=40 << 20),
        name="sum_blocks",
    )(target, items)


def turn_kernel(pieces_ref, out_ref):
    for l in range(OWN):
        out_ref[l] = pieces_ref[:, l].reshape(COLS, LANES).T


def turn_back(pieces):
    return pl.pallas_call(
        turn_kernel,
        in_specs=[pl.BlockSpec(memory_space=pltpu.VMEM)],
        out_specs=pl.BlockSpec(memory_space=pltpu.VMEM),
        out_shape=jax.ShapeDtypeStruct((OWN, LANES, COLS), jnp.bfloat16),
        compiler_params=pltpu.CompilerParams(vmem_limit_bytes=40 << 20),
        name="turn_back",
    )(pieces)


def total_of(*terms):
    acc = terms[0].astype(jnp.float32)
    for term in terms[1:]:
        acc = acc + term.astype(jnp.float32)
    return acc.astype(jnp.bfloat16)


def shift_z(k):
    return [(g, ((g // 2 + k) % N_Z) * 2 + g % 2) for g in range(N_GRP)]


def on_device(solved, e_blocks, block_mask, owner, local_id):
    mask = block_mask.reshape(SLOTS)
    labels = owner[0, :, 0] * OWN + local_id[0]
    sibling = [(g, g ^ 1) for g in range(N_GRP)]
    half = N_DOM // 2
    reduced = []
    for first, count in CHUNKS:
        own0, own1, own2, own3, other = product(solved, e_blocks, mask, first, count)
        twin = lax.ppermute(other, "grp", sibling)
        far_up = total_of(own2[:half], twin[2, :half])
        far_down = total_of(own2[half:], twin[2, half:])
        from_below = lax.ppermute(far_up, "grp", shift_z(1))
        from_above = lax.ppermute(far_down, "grp", shift_z(-1))
        up = jnp.concatenate(
            [total_of(own1[:half], twin[1, :half], from_below), total_of(own1[half:], twin[1, half:])]
        )
        down = jnp.concatenate(
            [total_of(own3[:half], twin[3, :half]), total_of(own3[half:], twin[3, half:], from_above)]
        )
        low = lax.ppermute(up, "grp", shift_z(1))
        high = lax.ppermute(down, "grp", shift_z(-1))
        reduced.append(total_of(own0, twin[0], low, high))
    everyone = jnp.broadcast_to(labels[None, :], (N_DOM, SLOTS))
    target = lax.all_to_all(everyone, "dom", split_axis=0, concat_axis=0, tiled=True)
    items = lax.all_to_all(
        jnp.concatenate(reduced, axis=1), "dom", split_axis=0, concat_axis=0, tiled=True
    )
    summed = sum_blocks(target.reshape(N_DOM * SLOTS), items)
    pieces = lax.all_to_all(
        summed.reshape(N_DOM, OWN, PIECE, LANES), "dom", split_axis=0, concat_axis=0, tiled=True
    )
    return turn_back(pieces)


def solution(mesh):
    in_specs = (
        P("dom", "grp", None),
        P("dom", None, "grp", None),
        P("dom", None, "grp"),
        P("dom", None, None),
        P("dom", None),
    )
    out_specs = P("dom", "grp", None)
    return jax.shard_map(
        on_device, mesh=mesh, in_specs=in_specs, out_specs=out_specs, check_vma=False
    )
```

time: 165 us -> 83.9 us (0.51)
  the two profiles are of different devices: /device:TPU:53 before, /device:TPU:0 now
where the time goes in v1:
time: 83.9 us; the launch traced here: 83.5 us
  starting transfers between devices  28.2 us (34%)
  waiting for transfers between devices  17.9 us (21%)
  Pallas kernels  14.6 us (17%)
  blocking collectives  13.5 us (16%)
  other arithmetic  6.06 us (7%)
  local copies, waits for them, and re-layouts  3.09 us (4%)
    all_to_all x1, blocking collectives, on_device(): lax.all_to_all(summed.reshape(N_DOM, OWN, PIECE, LANES), 'dom', split_axi...  13.5 us
    pallas_call x2, Pallas kernels, product(): pl.pallas_call(functools.partial(product_kernel, first), grid=(count,), i...  12.6 us
    all_to_all x1, waiting for transfers between devices, on_device(): lax.all_to_all(jnp.concatenate(reduced, axis=1), 'dom', split_axis=0, con...  11.7 us
    all_to_all x1, starting transfers between devices, on_device(): lax.all_to_all(everyone, 'dom', split_axis=0, concat_axis=0, tiled=True)  7.05 us
    all_to_all x1, starting transfers between devices, on_device(): lax.all_to_all(jnp.concatenate(reduced, axis=1), 'dom', split_axis=0, con...  6.22 us
    ppermute x2, starting transfers between devices, on_device(): from_above = lax.ppermute(far_down, 'grp', shift_z(-1))  4.74 us
    ppermute x2, starting transfers between devices, on_device(): high = lax.ppermute(down, 'grp', shift_z(-1))  3.59 us
    convert_element_type x6, other arithmetic, total_of(): return acc.astype(jnp.bfloat16)  3.53 us
  transfers between devices with their start and end apart: 12, of which 5 were waited for; matrix products, arithmetic and copies ran while one was open for 9% of the time, Pallas kernels for 8%

profile of v1, /device:TPU:0, one launch (start us, length us, event | category | flops | bytes accessed | tf_op | source)
XLA Modules:
  0.0 83.5 jit_solution(16881444628529830905)
XLA Ops:
  0.0 0.0 copy-start
  0.0 1.2 %copy-done = bf16[1,1024,512]{2,1,0:T(8,128)(2,1)S(1)} copy-done((bf16[1,1024,512]{2,1,0:T(8,128)(2,1)S(1)}, bf16[1,1024,512]{2,1,0:T(8,128)(2,1)}, u32[]{:S(2)}) %copy-start) | copy-done | bytes 1048600
  1.2 0.0 copy-start.1
  1.2 0.7 copy-done.1
  1.9 6.3 %product.2 = (bf16[16,3,32,128]{3,2,1,0:T(8,128)(2,1)S(1)}, bf16[16,3,32,128]{3,2,1,0:T(8,128)(2,1)S(1)}, bf16[16,3,32,128]{3,2,1,0:T(8,128)(2,1)S(1)}, bf16[16,...) custom-call(s32[6]{0:T(128)S(1)} %bitcast.79, bf16[1,1024,512]{2,1,0:T(8,128)(2,1)S(1)} %copy-done, ...), custom_call_target="tpu_custom_call" | custom-call | tf_op jit(solution)/shard_map/product/pallas_call | solution.py:50
  8.2 0.1 collective-permute-start
  8.3 6.3 %product.3 = (bf16[16,3,32,128]{3,2,1,0:T(8,128)(2,1)S(1)}, bf16[16,3,32,128]{3,2,1,0:T(8,128)(2,1)S(1)}, bf16[16,3,32,128]{3,2,1,0:T(8,128)(2,1)S(1)}, bf16[16,...) custom-call(s32[6]{0:T(128)S(1)} %bitcast.80, bf16[1,1024,512]{2,1,0:T(8,128)(2,1)S(1)} %copy-done, ...), custom_call_target="tpu_custom_call" | custom-call | tf_op jit(solution)/shard_map/product/pallas_call | solution.py:50
  14.6 0.6 collective-permute-start.5
  15.1 0.0 collective-permute-done
  15.1 0.0 copy-start.2
  15.1 0.1 fusion.19
  15.2 2.1 %collective-permute-start.1 = (bf16[8,3,32,128]{3,2,1,0:T(8,128)(2,1)S(1)}, bf16[8,3,32,128]{3,2,1,0:T(8,128)(2,1)S(1)}, u32[]{:S(2)}, u32[]{:S(2)}) collective-permute-start(bf16[8,3,32,128]{3,2,1,0:T(8,128)(2,1)S(1)} %get-tuple-element.27), channel_id=1, source_target_pairs={{0,2},{1,3},{2,4},{3,5},{4,6},{5,7},{6,0},{7,1},{8,10},{9,11},{10,... | collective-permute-start | bytes 589832 | tf_op jit(solution)/shard_map/ppermute | solution.py:134
  17.3 2.2 %collective-permute-start.3 = (bf16[8,3,32,128]{3,2,1,0:T(8,128)(2,1)S(1)}, bf16[8,3,32,128]{3,2,1,0:T(8,128)(2,1)S(1)}, u32[]{:S(2)}, u32[]{:S(2)}) collective-permute-start(bf16[8,3,32,128]{3,2,1,0:T(8,128)(2,1)S(1)} %get-tuple-element.28), channel_id=1, source_target_pairs={{0,6},{1,7},{2,0},{3,1},{4,2},{5,3},{6,4},{7,5},{8,14},{9,15},{10,... | collective-permute-start | bytes 589832 | tf_op jit(solution)/shard_map/ppermute | solution.py:135
  19.5 0.0 collective-permute-done.5
  19.5 0.1 fusion.11
  19.6 0.7 collective-permute-start.6
  20.4 2.6 %collective-permute-start.8 = (bf16[8,3,32,128]{3,2,1,0:T(8,128)(2,1)S(1)}, bf16[8,3,32,128]{3,2,1,0:T(8,128)(2,1)S(1)}, u32[]{:S(2)}, u32[]{:S(2)}) collective-permute-start(bf16[8,3,32,128]{3,2,1,0:T(8,128)(2,1)S(1)} %get-tuple-element.34), channel_id=1, source_target_pairs={{0,6},{1,7},{2,0},{3,1},{4,2},{5,3},{6,4},{7,5},{8,14},{9,15},{10,... | collective-permute-start | bytes 589832 | tf_op jit(solution)/shard_map/ppermute | solution.py:135
  22.9 2.2 %collective-permute-done.1 = bf16[8,3,32,128]{3,2,1,0:T(8,128)(2,1)S(1)} collective-permute-done((bf16[8,3,32,128]{3,2,1,0:T(8,128)(2,1)S(1)}, bf16[8,3,32,128]{3,2,1,0:T(8,128)(2,1)S(1)}, u32[]{:S(2)}, u32[]{:S(2)}) %collective-permute-start.1) | collective-permute-done | bytes 196640 | tf_op jit(solution)/shard_map/ppermute | solution.py:134
  25.1 0.0 collective-permute-done.3
  25.1 0.3 fusion.21
  25.4 0.0 copy-done.2
  25.5 1.5 %collective-permute-start.2 = (bf16[16,3,32,128]{3,2,1,0:T(8,128)(2,1)S(1)}, bf16[16,3,32,128]{3,2,1,0:T(8,128)(2,1)}, u32[]{:S(2)}, u32[]{:S(2)}) collective-permute-start(bf16[16,3,32,128]{3,2,1,0:T(8,128)(2,1)S(1)} %pad_maximum_fusion.1), channel_id=1, source_target_pairs={{0,2},{1,3},{2,4},{3,5},{4,6},{5,7},{6,0},{7,1},{8,10},{9,11},{10,... | collective-permute-start | bytes 1179656 | tf_op jit(solution)/shard_map/ppermute | solution.py:142
  27.0 1.9 %collective-permute-start.4 = (bf16[16,3,32,128]{3,2,1,0:T(8,128)(2,1)S(1)}, bf16[16,3,32,128]{3,2,1,0:T(8,128)(2,1)}, u32[]{:S(2)}, u32[]{:S(2)}) collective-permute-start(bf16[16,3,32,128]{3,2,1,0:T(8,128)(2,1)S(1)} %pad_maximum_fusion.2), channel_id=1, source_target_pairs={{0,6},{1,7},{2,0},{3,1},{4,2},{5,3},{6,4},{7,5},{8,14},{9,15},{10,... | collective-permute-start | bytes 1179656 | tf_op jit(solution)/shard_map/ppermute | solution.py:143
  28.9 0.3 collective-permute-done.6
  29.2 0.0 collective-permute-done.8
  29.2 0.0 copy-start.3
  29.2 0.0 copy-start.4
  29.2 0.3 fusion.13
  29.5 1.6 %collective-permute-start.7 = (bf16[16,3,32,128]{3,2,1,0:T(8,128)(2,1)S(1)}, bf16[16,3,32,128]{3,2,1,0:T(8,128)(2,1)}, u32[]{:S(2)}, u32[]{:S(2)}) collective-permute-start(bf16[16,3,32,128]{3,2,1,0:T(8,128)(2,1)S(1)} %pad_maximum_fusion.3), channel_id=1, source_target_pairs={{0,2},{1,3},{2,4},{3,5},{4,6},{5,7},{6,0},{7,1},{8,10},{9,11},{10,... | collective-permute-start | bytes 1179656 | tf_op jit(solution)/shard_map/ppermute | solution.py:142
  31.1 0.8 pad_maximum_fusion.4
  31.9 1.7 %collective-permute-start.9 = (bf16[16,3,32,128]{3,2,1,0:T(8,128)(2,1)}, bf16[16,3,32,128]{3,2,1,0:T(8,128)(2,1)}, u32[]{:S(2)}, u32[]{:S(2)}) collective-permute-start(bf16[16,3,32,128]{3,2,1,0:T(8,128)(2,1)} %pad_maximum_fusion.4), channel_id=1, source_target_pairs={{0,6},{1,7},{2,0},{3,1},{4,2},{5,3},{6,4},{7,5},{8,14},{9,15},{10,... | collective-permute-start | bytes 1179656 | tf_op jit(solution)/shard_map/ppermute | solution.py:143
  33.6 0.0 copy-done.3
  33.6 0.0 copy-done.4
  33.6 0.6 broadcast_in_dim.2
  34.2 7.1 %all-to-all-start = ((s32[16,1,6]{2,1,0:T(1,128)}), s32[16,1,6]{2,1,0:T(1,128)S(1)}, u32[]{:S(2)}, u32[]{:S(2)}) async-start(s32[16,1,6]{2,1,0:T(1,128)} %broadcast_in_dim.2), calls=%async_computation | async-start | bytes 16384 | tf_op jit(solution)/shard_map/all_to_all | solution.py:146
  41.3 0.0 collective-permute-done.2
  41.3 0.0 collective-permute-done.4
  41.3 1.4 %fusion.5 = bf16[16,3,32,128]{3,2,1,0:T(8,128)(2,1)S(1)} fusion(bf16[16,3,32,128]{3,2,1,0:T(8,128)(2,1)} %collective-permute-done.4, bf16[16,3,32,128]{3,2,1,0:T(8,128)(2,1)} %collective-permute-done.2, bf16[16,3,32,128]{3,2,1,0:T(8,128)(2,1)S(1)} %get-tuple-element.15, bf16[4,16,3,32,128]{4,3,2,1,0:T(8,128)(2,1)} %copy-done.2), kind=kLoop, calls=%fused_computation.8 | loop fusion | flops 1572864 | bytes 1966080 | tf_op jit(solution)/shard_map/convert_element_type | solution.py:116
  42.8 3.0 %collective-permute-done.7 = bf16[16,3,32,128]{3,2,1,0:T(8,128)(2,1)} collective-permute-done((bf16[16,3,32,128]{3,2,1,0:T(8,128)(2,1)S(1)}, bf16[16,3,32,128]{3,2,1,0:T(8,128)(2,1)}, u32[]{:S(2)}, u32[]{:S(2)}) %collective-permute-start.7) | collective-permute-done | bytes 393248 | tf_op jit(solution)/shard_map/ppermute | solution.py:142
  45.7 0.0 collective-permute-done.9
  45.7 1.3 %fusion.2 = bf16[16,3,32,128]{3,2,1,0:T(8,128)(2,1)S(1)} fusion(bf16[16,3,32,128]{3,2,1,0:T(8,128)(2,1)} %collective-permute-done.9, bf16[16,3,32,128]{3,2,1,0:T(8,128)(2,1)} %collective-permute-done.7, bf16[16,3,32,128]{3,2,1,0:T(8,128)(2,1)S(1)} %get-tuple-element.20, bf16[4,16,3,32,128]{4,3,2,1,0:T(8,128)(2,1)S(1)} %collective-permute-done.5), kind=kLoop, calls=%fused_computation.4 | loop fusion | flops 1572864 | bytes 1966080 | tf_op jit(solution)/shard_map/convert_element_type | solution.py:116
  47.0 1.0 %pad_maximum_fusion = bf16[16,6,32,128]{3,2,1,0:T(8,128)(2,1)} fusion(bf16[16,3,32,128]{3,2,1,0:T(8,128)(2,1)S(1)} %fusion.2, bf16[16,3,32,128]{3,2,1,0:T(8,128)(2,1)S(1)} %fusion.5), kind=kLoop, calls=%fused_computation | loop fusion | flops 393216 | bytes 1572864 | tf_op jit(solution)/shard_map/concatenate | solution.py:148
  48.0 0.8 all-to-all-done
  48.8 6.2 %all-to-all-start.1 = ((bf16[16,6,32,128]{3,2,1,0:T(8,128)(2,1)}), bf16[16,6,32,128]{3,2,1,0:T(8,128)(2,1)S(1)}, u32[]{:S(2)}, u32[]{:S(2)}) async-start(bf16[16,6,32,128]{3,2,1,0:T(8,128)(2,1)} %pad_maximum_fusion), calls=%async_computation.1 | async-start | bytes 1572864 | tf_op jit(solution)/shard_map/all_to_all | solution.py:147
  55.1 0.5 broadcast.21
  55.6 0.7 reduce.3
  56.3 0.1 reshape.56.target_ref
  56.3 11.7 %all-to-all-done.1.items_ref = bf16[16,6,32,128]{3,2,1,0:T(8,128)(2,1)S(1)} async-done(((bf16[16,6,32,128]{3,2,1,0:T(8,128)(2,1)}), bf16[16,6,32,128]{3,2,1,0:T(8,128)(2,1)S(1)}, u32[]{:S(2)}, u32[]{:S(2)}) %all-to-all-start.1) | async-done | bytes 786464 | tf_op jit(solution)/shard_map/all_to_all | solution.py:147
  68.0 1.0 %sum_blocks.1 = bf16[64,32,128]{2,1,0:T(8,128)(2,1)S(1)} custom-call(s32[96]{0:T(128)S(1)} %reshape.56.target_ref, bf16[16,6,32,128]{3,2,1,0:T(8,128)(2,1)S(1)} %all-to-all-done.1.items_ref), custom_call_target="tpu_custom_call" | custom-call | tf_op jit(solution)/shard_map/sum_blocks/pallas_call | solution.py:82
  69.0 13.5 %all_to_all.16.pieces_ref = bf16[16,4,32,128]{3,2,1,0:T(8,128)(2,1)S(1)} all-to-all(bf16[16,4,32,128]{3,2,1,0:T(8,128)(2,1)S(1)} %bitcast.78), channel_id=1, replica_groups=mesh['dom'=16,'grp'=8] {'dom'}, dimensions={0} | all-to-all | bytes 1048576 | tf_op jit(solution)/shard_map/all_to_all | solution.py:151
  82.5 1.0 %turn_back.1 = bf16[4,128,512]{2,1,0:T(8,128)(2,1)} custom-call(bf16[16,4,32,128]{3,2,1,0:T(8,128)(2,1)S(1)} %all_to_all.16.pieces_ref), custom_call_target="tpu_custom_call" | custom-call | tf_op jit(solution)/shard_map/turn_back/pallas_call | solution.py:102
  (4 shorter events, 0.1 us)
Async XLA Ops:
  0.0 1.2 %copy-start = (bf16[1,1024,512]{2,1,0:T(8,128)(2,1)S(1)}, bf16[1,1024,512]{2,1,0:T(8,128)(2,1)}, u32[]{:S(2)}) copy-start(bf16[1,1024,512]{2,1,0:T(8,128)(2,1)} %factor_ref.3) | copy-start | bytes 3145732
  1.2 0.7 copy-start.1
  8.2 7.0 %collective-permute-start = (bf16[4,16,3,32,128]{4,3,2,1,0:T(8,128)(2,1)S(1)}, bf16[4,16,3,32,128]{4,3,2,1,0:T(8,128)(2,1)S(1)}, u32[]{:S(2)}, u32[]{:S(2)}) collective-permute-start(bf16[4,16,3,32,128]{4,3,2,1,0:T(8,128)(2,1)S(1)} %get-tuple-element.16), channel_id=1, source_target_pairs={{0,1},{1,0},{2,3},{3,2},{4,5},{5,4},{6,7},{7,6},{8,9},{9,8},{10,11... | collective-permute-start | bytes 4718600 | tf_op jit(solution)/shard_map/ppermute | solution.py:131
  14.6 5.0 %collective-permute-start.5 = (bf16[4,16,3,32,128]{4,3,2,1,0:T(8,128)(2,1)S(1)}, bf16[4,16,3,32,128]{4,3,2,1,0:T(8,128)(2,1)S(1)}, u32[]{:S(2)}, u32[]{:S(2)}) collective-permute-start(bf16[4,16,3,32,128]{4,3,2,1,0:T(8,128)(2,1)S(1)} %get-tuple-element.21), channel_id=1, source_target_pairs={{0,1},{1,0},{2,3},{3,2},{4,5},{5,4},{6,7},{7,6},{8,9},{9,8},{10,11... | collective-permute-start | bytes 4718600 | tf_op jit(solution)/shard_map/ppermute | solution.py:131
  15.1 10.3 %copy-start.2 = (bf16[4,16,3,32,128]{4,3,2,1,0:T(8,128)(2,1)}, bf16[4,16,3,32,128]{4,3,2,1,0:T(8,128)(2,1)S(1)}, u32[]{:S(2)}) copy-start(bf16[4,16,3,32,128]{4,3,2,1,0:T(8,128)(2,1)S(1)} %collective-permute-done) | copy-start | bytes 4718596
  15.2 9.9 %collective-permute-start.1 = (bf16[8,3,32,128]{3,2,1,0:T(8,128)(2,1)S(1)}, bf16[8,3,32,128]{3,2,1,0:T(8,128)(2,1)S(1)}, u32[]{:S(2)}, u32[]{:S(2)}) collective-permute-start(bf16[8,3,32,128]{3,2,1,0:T(8,128)(2,1)S(1)} %get-tuple-element.27), channel_id=1, source_target_pairs={{0,2},{1,3},{2,4},{3,5},{4,6},{5,7},{6,0},{7,1},{8,10},{9,11},{10,... | collective-permute-start | bytes 589832 | tf_op jit(solution)/shard_map/ppermute | solution.py:134
  17.3 7.8 %collective-permute-start.3 = (bf16[8,3,32,128]{3,2,1,0:T(8,128)(2,1)S(1)}, bf16[8,3,32,128]{3,2,1,0:T(8,128)(2,1)S(1)}, u32[]{:S(2)}, u32[]{:S(2)}) collective-permute-start(bf16[8,3,32,128]{3,2,1,0:T(8,128)(2,1)S(1)} %get-tuple-element.28), channel_id=1, source_target_pairs={{0,6},{1,7},{2,0},{3,1},{4,2},{5,3},{6,4},{7,5},{8,14},{9,15},{10,... | collective-permute-start | bytes 589832 | tf_op jit(solution)/shard_map/ppermute | solution.py:135
  19.6 9.5 %collective-permute-start.6 = (bf16[8,3,32,128]{3,2,1,0:T(8,128)(2,1)S(1)}, bf16[8,3,32,128]{3,2,1,0:T(8,128)(2,1)S(1)}, u32[]{:S(2)}, u32[]{:S(2)}) collective-permute-start(bf16[8,3,32,128]{3,2,1,0:T(8,128)(2,1)S(1)} %get-tuple-element.33), channel_id=1, source_target_pairs={{0,2},{1,3},{2,4},{3,5},{4,6},{5,7},{6,0},{7,1},{8,10},{9,11},{10,... | collective-permute-start | bytes 589832 | tf_op jit(solution)/shard_map/ppermute | solution.py:134
  20.4 8.8 %collective-permute-start.8 = (bf16[8,3,32,128]{3,2,1,0:T(8,128)(2,1)S(1)}, bf16[8,3,32,128]{3,2,1,0:T(8,128)(2,1)S(1)}, u32[]{:S(2)}, u32[]{:S(2)}) collective-permute-start(bf16[8,3,32,128]{3,2,1,0:T(8,128)(2,1)S(1)} %get-tuple-element.34), channel_id=1, source_target_pairs={{0,6},{1,7},{2,0},{3,1},{4,2},{5,3},{6,4},{7,5},{8,14},{9,15},{10,... | collective-permute-start | bytes 589832 | tf_op jit(solution)/shard_map/ppermute | solution.py:135
  25.5 15.8 %collective-permute-start.2 = (bf16[16,3,32,128]{3,2,1,0:T(8,128)(2,1)S(1)}, bf16[16,3,32,128]{3,2,1,0:T(8,128)(2,1)}, u32[]{:S(2)}, u32[]{:S(2)}) collective-permute-start(bf16[16,3,32,128]{3,2,1,0:T(8,128)(2,1)S(1)} %pad_maximum_fusion.1), channel_id=1, source_target_pairs={{0,2},{1,3},{2,4},{3,5},{4,6},{5,7},{6,0},{7,1},{8,10},{9,11},{10,... | collective-permute-start | bytes 1179656 | tf_op jit(solution)/shard_map/ppermute | solution.py:142
  27.0 14.3 %collective-permute-start.4 = (bf16[16,3,32,128]{3,2,1,0:T(8,128)(2,1)S(1)}, bf16[16,3,32,128]{3,2,1,0:T(8,128)(2,1)}, u32[]{:S(2)}, u32[]{:S(2)}) collective-permute-start(bf16[16,3,32,128]{3,2,1,0:T(8,128)(2,1)S(1)} %pad_maximum_fusion.2), channel_id=1, source_target_pairs={{0,6},{1,7},{2,0},{3,1},{4,2},{5,3},{6,4},{7,5},{8,14},{9,15},{10,... | collective-permute-start | bytes 1179656 | tf_op jit(solution)/shard_map/ppermute | solution.py:143
  29.2 4.4 %copy-start.3 = (s32[1,6]{1,0:T(1,128)S(1)}, s32[1,6]{1,0:T(1,128)}, u32[]{:S(2)}) copy-start(s32[1,6]{1,0:T(1,128)} %param.9) | copy-start | bytes 76
  29.2 4.4 %copy-start.4 = (s32[1,6,1]{1,2,0:T(1,128)S(1)}, s32[1,6,1]{1,2,0:T(1,128)}, u32[]{:S(2)}) copy-start(s32[1,6,1]{1,2,0:T(1,128)} %param.8) | copy-start | bytes 76
  29.5 16.2 %collective-permute-start.7 = (bf16[16,3,32,128]{3,2,1,0:T(8,128)(2,1)S(1)}, bf16[16,3,32,128]{3,2,1,0:T(8,128)(2,1)}, u32[]{:S(2)}, u32[]{:S(2)}) collective-permute-start(bf16[16,3,32,128]{3,2,1,0:T(8,128)(2,1)S(1)} %pad_maximum_fusion.3), channel_id=1, source_target_pairs={{0,2},{1,3},{2,4},{3,5},{4,6},{5,7},{6,0},{7,1},{8,10},{9,11},{10,... | collective-permute-start | bytes 1179656 | tf_op jit(solution)/shard_map/ppermute | solution.py:142
  31.9 13.8 %collective-permute-start.9 = (bf16[16,3,32,128]{3,2,1,0:T(8,128)(2,1)}, bf16[16,3,32,128]{3,2,1,0:T(8,128)(2,1)}, u32[]{:S(2)}, u32[]{:S(2)}) collective-permute-start(bf16[16,3,32,128]{3,2,1,0:T(8,128)(2,1)} %pad_maximum_fusion.4), channel_id=1, source_target_pairs={{0,6},{1,7},{2,0},{3,1},{4,2},{5,3},{6,4},{7,5},{8,14},{9,15},{10,... | collective-permute-start | bytes 1179656 | tf_op jit(solution)/shard_map/ppermute | solution.py:143
  34.2 14.6 %all-to-all-start = ((s32[16,1,6]{2,1,0:T(1,128)}), s32[16,1,6]{2,1,0:T(1,128)S(1)}, u32[]{:S(2)}, u32[]{:S(2)}) async-start(s32[16,1,6]{2,1,0:T(1,128)} %broadcast_in_dim.2), calls=%async_computation | async-start | bytes 16384 | tf_op jit(solution)/shard_map/all_to_all | solution.py:146
  48.8 19.2 %all-to-all-start.1 = ((bf16[16,6,32,128]{3,2,1,0:T(8,128)(2,1)}), bf16[16,6,32,128]{3,2,1,0:T(8,128)(2,1)S(1)}, u32[]{:S(2)}, u32[]{:S(2)}) async-start(bf16[16,6,32,128]{3,2,1,0:T(8,128)(2,1)} %pad_maximum_fusion), calls=%async_computation.1 | async-start | bytes 1572864 | tf_op jit(solution)/shard_map/all_to_all | solution.py:147

commit v2 on v1

v2 whole, which is shorter than its diff:
```python
import functools
import jax
import jax.numpy as jnp
from jax import lax
from jax.experimental import pallas as pl
from jax.experimental.pallas import tpu as pltpu
from jax.sharding import PartitionSpec as P

BLK = 1024
COLS = 512
SLOTS = 6
OWN = 4
N_DOM = 16
N_GRP = 8
N_Z = 4
LANES = BLK // N_GRP
PIECE = COLS // N_DOM
TAIL = 8
CHUNKS = ((0, 4), (4, 2))
CONTRACT_ROWS = (((0,), (0,)), ((), ()))
VMEM_LIMIT = 24 << 20


def whole_vmem():
    return pl.BlockSpec(memory_space=pltpu.VMEM)


def whole_smem():
    return pl.BlockSpec(memory_space=pltpu.SMEM)


def plane_and_core():
    group = lax.axis_index("grp")
    return lax.div(group, 2), lax.rem(group, 2)


def product_kernel(first, mask, factor, *refs):
    *couplings, own, other = refs
    core = plane_and_core()[1]
    slot = pl.program_id(0)
    present = mask[first + slot].astype(jnp.float32).astype(jnp.bfloat16)
    for k, coupling in enumerate(couplings):
        both = lax.dot_general(
            factor[0], coupling[...], CONTRACT_ROWS, preferred_element_type=jnp.float32
        )
        both = both.astype(jnp.bfloat16) * present
        low, high = both[:, :LANES], both[:, LANES:]
        own[k, :, slot] = jnp.where(core == 0, low, high).reshape(N_DOM, PIECE, LANES)
        other[k, :, slot] = jnp.where(core == 0, high, low).reshape(N_DOM, PIECE, LANES)


def coupling_spec(first, k):
    def block(s):
        return 0, first + s, 0, lax.rem(plane_and_core()[0] + k, N_Z)

    return pl.BlockSpec((None, None, BLK, 2 * LANES), block)


def product(solved, e_blocks, mask, first, count):
    shape = jax.ShapeDtypeStruct((N_Z, N_DOM, count, PIECE, LANES), jnp.bfloat16)
    return pl.pallas_call(
        functools.partial(product_kernel, first),
        grid=(count,),
        in_specs=[whole_smem(), pl.BlockSpec((1, BLK, COLS), lambda s: (0, 0, 0))]
        + [coupling_spec(first, k) for k in range(N_Z)],
        out_specs=[whole_vmem()] * 2,
        out_shape=[shape] * 2,
        compiler_params=pltpu.CompilerParams(vmem_limit_bytes=VMEM_LIMIT),
        name="product",
    )(mask, solved, *[e_blocks] * N_Z)


def finish_kernel(owner, local, *refs):
    *parts, out = refs
    for (first, count), (own, twin, low, high) in zip(CHUNKS, zip(*[iter(parts)] * 4)):
        for s in range(count):
            total = (
                own[0, :, s].astype(jnp.float32)
                + twin[0, :, s].astype(jnp.float32)
                + low[:, s].astype(jnp.float32)
                + high[:, s].astype(jnp.float32)
            )
            rows = slice((first + s) * PIECE, (first + s + 1) * PIECE)
            out[:, rows] = total.astype(jnp.bfloat16)
    lane = lax.broadcasted_iota(jnp.int32, (TAIL, LANES), 1)
    labels = jnp.zeros((TAIL, LANES), jnp.int32)
    for s in range(SLOTS):
        labels = jnp.where(lane == s, owner[s] * OWN + local[s], labels)
    labels = labels.astype(jnp.float32).astype(jnp.bfloat16)
    out[:, SLOTS * PIECE :] = jnp.broadcast_to(labels[None], (N_DOM, TAIL, LANES))


def finish(owner, local_id, parts):
    return pl.pallas_call(
        finish_kernel,
        in_specs=[whole_smem()] * 2 + [whole_vmem()] * len(parts),
        out_specs=whole_vmem(),
        out_shape=jax.ShapeDtypeStruct((N_DOM, SLOTS * PIECE + TAIL, LANES), jnp.bfloat16),
        compiler_params=pltpu.CompilerParams(vmem_limit_bytes=VMEM_LIMIT),
        name="finish",
    )(owner, local_id, *parts)


def sum_kernel(target, items, out, total):
    total[...] = jnp.zeros_like(total)

    def add(i, _):
        for s in range(SLOTS):
            t = target[i * SLOTS + s]
            rows = items[i, s * PIECE : (s + 1) * PIECE]
            total[t] = total[t] + rows.astype(jnp.float32)
        return 0

    lax.fori_loop(0, N_DOM, add, 0)
    out[...] = total[...].astype(jnp.bfloat16)


def sum_blocks(target, items):
    shape = (N_DOM * OWN, PIECE, LANES)
    return pl.pallas_call(
        sum_kernel,
        in_specs=[whole_smem(), whole_vmem()],
        out_specs=whole_vmem(),
        out_shape=jax.ShapeDtypeStruct(shape, jnp.bfloat16),
        scratch_shapes=[pltpu.VMEM(shape, jnp.float32)],
        compiler_params=pltpu.CompilerParams(vmem_limit_bytes=VMEM_LIMIT),
        name="sum_blocks",
    )(target, items)


def turn_kernel(pieces, out):
    for l in range(OWN):
        out[l] = pieces[:, l].reshape(COLS, LANES).T


def turn_back(pieces):
    return pl.pallas_call(
        turn_kernel,
        in_specs=[whole_vmem()],
        out_specs=whole_vmem(),
        out_shape=jax.ShapeDtypeStruct((OWN, LANES, COLS), jnp.bfloat16),
        compiler_params=pltpu.CompilerParams(vmem_limit_bytes=VMEM_LIMIT),
        name="turn_back",
    )(pieces)


def total_of(*terms):
    acc = terms[0].astype(jnp.float32)
    for term in terms[1:]:
        acc = acc + term.astype(jnp.float32)
    return acc.astype(jnp.bfloat16)


def shift_z(k):
    return [(g, ((g // 2 + k) % N_Z) * 2 + g % 2) for g in range(N_GRP)]


def exchange(x):
    return lax.all_to_all(x, "dom", split_axis=0, concat_axis=0, tiled=True)


def on_device(solved, e_blocks, block_mask, owner, local_id):
    solved = pltpu.with_memory_space_constraint(solved, pltpu.HBM)
    e_blocks = pltpu.with_memory_space_constraint(e_blocks, pltpu.HBM)
    mask = pltpu.with_memory_space_constraint(block_mask.reshape(SLOTS), pltpu.HBM)
    sibling = [(g, g ^ 1) for g in range(N_GRP)]
    half = N_DOM // 2
    parts = []
    for first, count in CHUNKS:
        own, other = product(solved, e_blocks, mask, first, count)
        twin = lax.ppermute(other, "grp", sibling)
        far_up = total_of(own[2, :half], twin[2, :half])
        far_down = total_of(own[2, half:], twin[2, half:])
        from_below = lax.ppermute(far_up, "grp", shift_z(1))
        from_above = lax.ppermute(far_down, "grp", shift_z(-1))
        up = jnp.concatenate(
            [total_of(own[1, :half], twin[1, :half], from_below), total_of(own[1, half:], twin[1, half:])]
        )
        down = jnp.concatenate(
            [total_of(own[3, :half], twin[3, :half]), total_of(own[3, half:], twin[3, half:], from_above)]
        )
        low = lax.ppermute(up, "grp", shift_z(1))
        high = lax.ppermute(down, "grp", shift_z(-1))
        parts += [own, twin, low, high]
    items = exchange(finish(owner.reshape(SLOTS), local_id.reshape(SLOTS), parts))
    target = items[:, SLOTS * PIECE, :SLOTS].astype(jnp.int32)
    summed = sum_blocks(target.reshape(N_DOM * SLOTS), items)
    pieces = exchange(summed.reshape(N_DOM, OWN, PIECE, LANES))
    return turn_back(pieces)


def solution(mesh):
    in_specs = (
        P("dom", "grp", None),
        P("dom", None, "grp", None),
        P("dom", None, "grp"),
        P("dom", None, None),
        P("dom", None),
    )
    out_specs = P("dom", "grp", None)
    return jax.shard_map(
        on_device, mesh=mesh, in_specs=in_specs, out_specs=out_specs, check_vma=False
    )
```

time: 83.9 us -> 81.9 us (0.976)
  blocking collectives: 13.5 us -> 31.8 us
  starting transfers between devices: 28.2 us -> 14.8 us
  other arithmetic: 6.06 us -> 1.05 us
  local copies, waits for them, and re-layouts: 3.09 us -> 0.1 us
    all_to_all x1 -> x2, blocking collectives: 13.5 us -> 31.8 us  [exchange(): return lax.all_to_all(x, 'dom', split_axis=0, concat_axis=0, tiled=True)]
    all_to_all x2 -> x0, starting transfers between devices: 13.3 us -> none  [the longest x1 7.05 us: on_device(): lax.all_to_all(everyone, 'dom', split_axis=0, concat_axis=0, tiled=True)]
    all_to_all x2 -> x0, waiting for transfers between devices: 12.5 us -> none  [the longest x1 11.7 us: on_device(): lax.all_to_all(jnp.concatenate(reduced, axis=1), 'dom', split_axis=0, con...]
    ppermute x2, waiting for transfers between devices: 2.97 us -> 11.5 us  [on_device(): low = lax.ppermute(up, 'grp', shift_z(1))]
    ppermute x2, waiting for transfers between devices: 0.01 us -> 3.17 us  [on_device(): from_above = lax.ppermute(far_down, 'grp', shift_z(-1))]
    ppermute x2, starting transfers between devices: 3.59 us -> 6.57 us  [on_device(): high = lax.ppermute(down, 'grp', shift_z(-1))]
    ppermute x2, starting transfers between devices: 3.09 us -> 0.15 us  [on_device(): low = lax.ppermute(up, 'grp', shift_z(1))]
    ppermute x2, starting transfers between devices: 2.84 us -> 0.01 us  [on_device(): from_below = lax.ppermute(far_up, 'grp', shift_z(1))]
  transfers between devices with their start and end apart: 12 -> 10, of which waited for: 5 -> 3; matrix products, arithmetic and copies ran while one was open for 9% -> 1% of each run, Pallas kernels for 8% -> 6%
where the time goes in v2:
time: 81.9 us; the launch traced here: 81.7 us
  blocking collectives  31.8 us (39%)
  waiting for transfers between devices  18.4 us (22%)
  Pallas kernels  15.3 us (19%)
  starting transfers between devices  14.8 us (18%)
  other arithmetic  1.05 us (1%)
    all_to_all x2, blocking collectives, exchange(): return lax.all_to_all(x, 'dom', split_axis=0, concat_axis=0, tiled=True)  31.8 us
    pallas_call x2, Pallas kernels, product(): pl.pallas_call(functools.partial(product_kernel, first), grid=(count,), i...  12.3 us
    ppermute x2, waiting for transfers between devices, on_device(): low = lax.ppermute(up, 'grp', shift_z(1))  11.5 us
    ppermute x2, starting transfers between devices, on_device(): from_above = lax.ppermute(far_down, 'grp', shift_z(-1))  7.5 us
    ppermute x2, starting transfers between devices, on_device(): high = lax.ppermute(down, 'grp', shift_z(-1))  6.57 us
    ppermute x2, waiting for transfers between devices, on_device(): from_below = lax.ppermute(far_up, 'grp', shift_z(1))  3.73 us
    ppermute x2, waiting for transfers between devices, on_device(): from_above = lax.ppermute(far_down, 'grp', shift_z(-1))  3.17 us
  transfers between devices with their start and end apart: 10, of which 3 were waited for; matrix products, arithmetic and copies ran while one was open for 1% of the time, Pallas kernels for 6%

profile of v2, /device:TPU:0, one launch (start us, length us, event | category | flops | bytes accessed | tf_op | source)
XLA Modules:
  0.0 81.7 jit_solution(10619372140088258650)
XLA Ops:
  0.0 7.6 %product.2 = (bf16[4,16,4,32,128]{4,3,2,1,0:T(8,128)(2,1)S(1)}, bf16[4,16,4,32,128]{4,3,2,1,0:T(8,128)(2,1)S(1)}) custom-call(s32[6]{0:T(128)} %bitcast.39, bf16[1,1024,512]{2,1,0:T(8,128)(2,1)} %factor.3, bf16[1,6,1024,1024]{3,2,1,0:T(8,128)(2,1)} %refs_3_.3, bf16[1,6,1024,1024]{3,2,1,0:T(8,128)(2,1)} %refs_3_.3, bf16[1,6,1024,1024]{3,2,1,0:T(8,128)(2,1)} %refs_3_.3, ...), custom_call_target="tpu_custom_call" | custom-call | tf_op jit(solution)/shard_map/product/pallas_call | solution.py:61
  7.6 0.1 collective-permute-start
  7.7 4.7 %product.3 = (bf16[4,16,2,32,128]{4,3,2,1,0:T(8,128)(2,1)S(1)}, bf16[4,16,2,32,128]{4,3,2,1,0:T(8,128)(2,1)S(1)}) custom-call(s32[6]{0:T(128)} %bitcast.40, bf16[1,1024,512]{2,1,0:T(8,128)(2,1)} %factor.3, bf16[1,6,1024,1024]{3,2,1,0:T(8,128)(2,1)} %refs_3_.3, bf16[1,6,1024,1024]{3,2,1,0:T(8,128)(2,1)} %refs_3_.3, bf16[1,6,1024,1024]{3,2,1,0:T(8,128)(2,1)} %refs_3_.3, ...), custom_call_target="tpu_custom_call" | custom-call | tf_op jit(solution)/shard_map/product/pallas_call | solution.py:61
  12.5 0.5 collective-permute-start.5
  13.0 0.0 collective-permute-done.refs_1_
  13.0 0.4 fusion.4
  13.3 4.2 %collective-permute-start.3 = (bf16[8,4,32,128]{3,2,1,0:T(8,128)(2,1)S(1)}, bf16[8,4,32,128]{3,2,1,0:T(8,128)(2,1)S(1)}, u32[]{:S(2)}, u32[]{:S(2)}) collective-permute-start(bf16[8,4,32,128]{3,2,1,0:T(8,128)(2,1)S(1)} %get-tuple-element.14), channel_id=1, source_target_pairs={{0,6},{1,7},{2,0},{3,1},{4,2},{5,3},{6,4},{7,5},{8,14},{9,15},{10,... | collective-permute-start | bytes 786440 | tf_op jit(solution)/shard_map/ppermute | solution.py:175
  17.5 0.0 collective-permute-start.1
  17.5 0.0 collective-permute-done.5.refs_5_
  17.5 0.2 fusion.10
  17.7 3.3 %collective-permute-start.8 = (bf16[8,2,32,128]{3,2,1,0:T(8,128)(2,1)S(1)}, bf16[8,2,32,128]{3,2,1,0:T(8,128)(2,1)S(1)}, u32[]{:S(2)}, u32[]{:S(2)}) collective-permute-start(bf16[8,2,32,128]{3,2,1,0:T(8,128)(2,1)S(1)} %get-tuple-element.20), channel_id=1, source_target_pairs={{0,6},{1,7},{2,0},{3,1},{4,2},{5,3},{6,4},{7,5},{8,14},{9,15},{10,... | collective-permute-start | bytes 393224 | tf_op jit(solution)/shard_map/ppermute | solution.py:175
  21.0 0.0 collective-permute-start.6
  21.0 3.2 %collective-permute-done.3 = bf16[8,4,32,128]{3,2,1,0:T(8,128)(2,1)S(1)} collective-permute-done((bf16[8,4,32,128]{3,2,1,0:T(8,128)(2,1)S(1)}, bf16[8,4,32,128]{3,2,1,0:T(8,128)(2,1)S(1)}, u32[]{:S(2)}, u32[]{:S(2)}) %collective-permute-start.3) | collective-permute-done | bytes 262176 | tf_op jit(solution)/shard_map/ppermute | solution.py:175
  24.2 3.7 %collective-permute-done.1 = bf16[8,4,32,128]{3,2,1,0:T(8,128)(2,1)S(1)} collective-permute-done((bf16[8,4,32,128]{3,2,1,0:T(8,128)(2,1)S(1)}, bf16[8,4,32,128]{3,2,1,0:T(8,128)(2,1)S(1)}, u32[]{:S(2)}, u32[]{:S(2)}) %collective-permute-start.1) | collective-permute-done | bytes 262176 | tf_op jit(solution)/shard_map/ppermute | solution.py:174
  27.9 0.2 fusion
  28.1 0.0 copy-start
  28.2 0.0 copy-start.1
  28.2 0.1 collective-permute-start.2
  28.4 3.3 %collective-permute-start.4 = (bf16[16,4,32,128]{3,2,1,0:T(8,128)(2,1)S(1)}, bf16[16,4,32,128]{3,2,1,0:T(8,128)(2,1)S(1)}, u32[]{:S(2)}, u32[]{:S(2)}) collective-permute-start(bf16[16,4,32,128]{3,2,1,0:T(8,128)(2,1)S(1)} %pad_maximum_fusion.1), channel_id=1, source_target_pairs={{0,6},{1,7},{2,0},{3,1},{4,2},{5,3},{6,4},{7,5},{8,14},{9,15},{10,... | collective-permute-start | bytes 1572872 | tf_op jit(solution)/shard_map/ppermute | solution.py:183
  31.7 0.0 collective-permute-done.8
  31.7 0.0 collective-permute-done.6
  31.7 0.1 fusion.6
  31.8 0.1 collective-permute-start.7
  31.9 3.3 %collective-permute-start.9 = (bf16[16,2,32,128]{3,2,1,0:T(8,128)(2,1)S(1)}, bf16[16,2,32,128]{3,2,1,0:T(8,128)(2,1)S(1)}, u32[]{:S(2)}, u32[]{:S(2)}) collective-permute-start(bf16[16,2,32,128]{3,2,1,0:T(8,128)(2,1)S(1)} %pad_maximum_fusion.3), channel_id=1, source_target_pairs={{0,6},{1,7},{2,0},{3,1},{4,2},{5,3},{6,4},{7,5},{8,14},{9,15},{10,... | collective-permute-start | bytes 786440 | tf_op jit(solution)/shard_map/ppermute | solution.py:183
  35.2 11.5 %collective-permute-done.7.refs_6_ = bf16[16,2,32,128]{3,2,1,0:T(8,128)(2,1)S(1)} collective-permute-done((bf16[16,2,32,128]{3,2,1,0:T(8,128)(2,1)S(1)}, bf16[16,2,32,128]{3,2,1,0:T(8,128)(2,1)S(1)}, u32[]{:S(2)}, u32[]{:S(2)}) %collective-permute-start.7) | collective-permute-done | bytes 262176 | tf_op jit(solution)/shard_map/ppermute | solution.py:182
  46.7 0.0 collective-permute-done.9.refs_7_
  46.7 0.0 collective-permute-done.2.refs_2_
  46.7 0.0 collective-permute-done.4.refs_3_
  46.7 0.0 copy-done
  46.7 0.0 copy-done.1
  46.8 0.9 %finish.1 = bf16[16,200,128]{2,1,0:T(8,128)(2,1)S(1)} custom-call(s32[6]{0:T(128)S(1)} %bitcast.37, s32[6]{0:T(128)S(1)} %bitcast.38, bf16[4,16,4,32,128]{4,3,2,1,0:T(8,128)(2,1)S(1)} %get-tuple-element.9.refs_0_, bf16[4,16,4,32,128]{4,3,2,1,0:T(8,128)(2,1)S(1)} %collective-permute-done.refs_1_, bf16[16,4,32,128]{3,2,1,0:T(8,128)(2,1)S(1)} %collective-permute-done.2.refs_2_, ...), custom_call_target="tpu_custom_call" | custom-call | tf_op jit(solution)/shard_map/finish/pallas_call | solution.py:94
  47.7 18.3 %all_to_all.10.items = bf16[16,200,128]{2,1,0:T(8,128)(2,1)S(1)} all-to-all(bf16[16,200,128]{2,1,0:T(8,128)(2,1)S(1)} %finish.1), channel_id=1, replica_groups=mesh['dom'=16,'grp'=8] {'dom'}, dimensions={0} | all-to-all | bytes 1638400 | tf_op jit(solution)/shard_map/all_to_all | solution.py:159
  66.0 0.1 reshape.64.target
  66.1 1.0 %sum_blocks.1 = bf16[64,32,128]{2,1,0:T(8,128)(2,1)S(1)} custom-call(s32[96]{0:T(128)S(1)} %reshape.64.target, bf16[16,200,128]{2,1,0:T(8,128)(2,1)S(1)} %all_to_all.10.items), custom_call_target="tpu_custom_call" | custom-call | tf_op jit(solution)/shard_map/sum_blocks/pallas_call | solution.py:120
  67.2 13.5 %all_to_all.11.pieces = bf16[16,4,32,128]{3,2,1,0:T(8,128)(2,1)S(1)} all-to-all(bf16[16,4,32,128]{3,2,1,0:T(8,128)(2,1)S(1)} %bitcast.36), channel_id=1, replica_groups=mesh['dom'=16,'grp'=8] {'dom'}, dimensions={0} | all-to-all | bytes 1048576 | tf_op jit(solution)/shard_map/all_to_all | solution.py:159
  80.7 1.0 %turn_back.1 = bf16[4,128,512]{2,1,0:T(8,128)(2,1)} custom-call(bf16[16,4,32,128]{3,2,1,0:T(8,128)(2,1)S(1)} %all_to_all.11.pieces), custom_call_target="tpu_custom_call" | custom-call | tf_op jit(solution)/shard_map/turn_back/pallas_call | solution.py:137
  (5 shorter events, 0.2 us)
Async XLA Ops:
  7.6 5.3 %collective-permute-start = (bf16[4,16,4,32,128]{4,3,2,1,0:T(8,128)(2,1)S(1)}, bf16[4,16,4,32,128]{4,3,2,1,0:T(8,128)(2,1)S(1)}, u32[]{:S(2)}, u32[]{:S(2)}) collective-permute-start(bf16[4,16,4,32,128]{4,3,2,1,0:T(8,128)(2,1)S(1)} %get-tuple-element.10), channel_id=1, source_target_pairs={{0,1},{1,0},{2,3},{3,2},{4,5},{5,4},{6,7},{7,6},{8,9},{9,8},{10,11... | collective-permute-start | bytes 6291464 | tf_op jit(solution)/shard_map/ppermute | solution.py:171
  12.5 5.1 %collective-permute-start.5 = (bf16[4,16,2,32,128]{4,3,2,1,0:T(8,128)(2,1)S(1)}, bf16[4,16,2,32,128]{4,3,2,1,0:T(8,128)(2,1)S(1)}, u32[]{:S(2)}, u32[]{:S(2)}) collective-permute-start(bf16[4,16,2,32,128]{4,3,2,1,0:T(8,128)(2,1)S(1)} %get-tuple-element.12), channel_id=1, source_target_pairs={{0,1},{1,0},{2,3},{3,2},{4,5},{5,4},{6,7},{7,6},{8,9},{9,8},{10,11... | collective-permute-start | bytes 3145736 | tf_op jit(solution)/shard_map/ppermute | solution.py:171
  13.3 10.9 %collective-permute-start.3 = (bf16[8,4,32,128]{3,2,1,0:T(8,128)(2,1)S(1)}, bf16[8,4,32,128]{3,2,1,0:T(8,128)(2,1)S(1)}, u32[]{:S(2)}, u32[]{:S(2)}) collective-permute-start(bf16[8,4,32,128]{3,2,1,0:T(8,128)(2,1)S(1)} %get-tuple-element.14), channel_id=1, source_target_pairs={{0,6},{1,7},{2,0},{3,1},{4,2},{5,3},{6,4},{7,5},{8,14},{9,15},{10,... | collective-permute-start | bytes 786440 | tf_op jit(solution)/shard_map/ppermute | solution.py:175
  17.5 10.4 %collective-permute-start.1 = (bf16[8,4,32,128]{3,2,1,0:T(8,128)(2,1)S(1)}, bf16[8,4,32,128]{3,2,1,0:T(8,128)(2,1)S(1)}, u32[]{:S(2)}, u32[]{:S(2)}) collective-permute-start(bf16[8,4,32,128]{3,2,1,0:T(8,128)(2,1)S(1)} %get-tuple-element.16), channel_id=1, source_target_pairs={{0,2},{1,3},{2,4},{3,5},{4,6},{5,7},{6,0},{7,1},{8,10},{9,11},{10,... | collective-permute-start | bytes 786440 | tf_op jit(solution)/shard_map/ppermute | solution.py:174
  17.7 13.9 %collective-permute-start.8 = (bf16[8,2,32,128]{3,2,1,0:T(8,128)(2,1)S(1)}, bf16[8,2,32,128]{3,2,1,0:T(8,128)(2,1)S(1)}, u32[]{:S(2)}, u32[]{:S(2)}) collective-permute-start(bf16[8,2,32,128]{3,2,1,0:T(8,128)(2,1)S(1)} %get-tuple-element.20), channel_id=1, source_target_pairs={{0,6},{1,7},{2,0},{3,1},{4,2},{5,3},{6,4},{7,5},{8,14},{9,15},{10,... | collective-permute-start | bytes 393224 | tf_op jit(solution)/shard_map/ppermute | solution.py:175
  21.0 10.6 %collective-permute-start.6 = (bf16[8,2,32,128]{3,2,1,0:T(8,128)(2,1)S(1)}, bf16[8,2,32,128]{3,2,1,0:T(8,128)(2,1)S(1)}, u32[]{:S(2)}, u32[]{:S(2)}) collective-permute-start(bf16[8,2,32,128]{3,2,1,0:T(8,128)(2,1)S(1)} %get-tuple-element.22), channel_id=1, source_target_pairs={{0,2},{1,3},{2,4},{3,5},{4,6},{5,7},{6,0},{7,1},{8,10},{9,11},{10,... | collective-permute-start | bytes 393224 | tf_op jit(solution)/shard_map/ppermute | solution.py:174
  28.1 18.6 %copy-start = (s32[1,6,1]{1,2,0:T(1,128)S(1)}, s32[1,6,1]{1,2,0:T(1,128)}, u32[]{:S(2)}) copy-start(s32[1,6,1]{1,2,0:T(1,128)} %param.8) | copy-start | bytes 76
  28.2 18.6 %copy-start.1 = (s32[1,6]{1,0:T(1,128)S(1)}, s32[1,6]{1,0:T(1,128)}, u32[]{:S(2)}) copy-start(s32[1,6]{1,0:T(1,128)} %param.9) | copy-start | bytes 76
  28.2 18.5 %collective-permute-start.2 = (bf16[16,4,32,128]{3,2,1,0:T(8,128)(2,1)S(1)}, bf16[16,4,32,128]{3,2,1,0:T(8,128)(2,1)S(1)}, u32[]{:S(2)}, u32[]{:S(2)}) collective-permute-start(bf16[16,4,32,128]{3,2,1,0:T(8,128)(2,1)S(1)} %pad_maximum_fusion), channel_id=1, source_target_pairs={{0,2},{1,3},{2,4},{3,5},{4,6},{5,7},{6,0},{7,1},{8,10},{9,11},{10,... | collective-permute-start | bytes 1572872 | tf_op jit(solution)/shard_map/ppermute | solution.py:182
  28.4 18.4 %collective-permute-start.4 = (bf16[16,4,32,128]{3,2,1,0:T(8,128)(2,1)S(1)}, bf16[16,4,32,128]{3,2,1,0:T(8,128)(2,1)S(1)}, u32[]{:S(2)}, u32[]{:S(2)}) collective-permute-start(bf16[16,4,32,128]{3,2,1,0:T(8,128)(2,1)S(1)} %pad_maximum_fusion.1), channel_id=1, source_target_pairs={{0,6},{1,7},{2,0},{3,1},{4,2},{5,3},{6,4},{7,5},{8,14},{9,15},{10,... | collective-permute-start | bytes 1572872 | tf_op jit(solution)/shard_map/ppermute | solution.py:183
  31.8 14.9 %collective-permute-start.7 = (bf16[16,2,32,128]{3,2,1,0:T(8,128)(2,1)S(1)}, bf16[16,2,32,128]{3,2,1,0:T(8,128)(2,1)S(1)}, u32[]{:S(2)}, u32[]{:S(2)}) collective-permute-start(bf16[16,2,32,128]{3,2,1,0:T(8,128)(2,1)S(1)} %pad_maximum_fusion.2), channel_id=1, source_target_pairs={{0,2},{1,3},{2,4},{3,5},{4,6},{5,7},{6,0},{7,1},{8,10},{9,11},{10,... | collective-permute-start | bytes 786440 | tf_op jit(solution)/shard_map/ppermute | solution.py:182
  31.9 14.8 %collective-permute-start.9 = (bf16[16,2,32,128]{3,2,1,0:T(8,128)(2,1)S(1)}, bf16[16,2,32,128]{3,2,1,0:T(8,128)(2,1)S(1)}, u32[]{:S(2)}, u32[]{:S(2)}) collective-permute-start(bf16[16,2,32,128]{3,2,1,0:T(8,128)(2,1)S(1)} %pad_maximum_fusion.3), channel_id=1, source_target_pairs={{0,6},{1,7},{2,0},{3,1},{4,2},{5,3},{6,4},{7,5},{8,14},{9,15},{10,... | collective-permute-start | bytes 786440 | tf_op jit(solution)/shard_map/ppermute | solution.py:183

commit v3 on v2

--- a/solution.py
+++ b/solution.py
@@ -70,35 +70,38 @@
     )(mask, solved, *[e_blocks] * N_Z)
 
 
-def finish_kernel(owner, local, *refs):
-    *parts, out = refs
-    for (first, count), (own, twin, low, high) in zip(CHUNKS, zip(*[iter(parts)] * 4)):
-        for s in range(count):
-            total = (
-                own[0, :, s].astype(jnp.float32)
-                + twin[0, :, s].astype(jnp.float32)
-                + low[:, s].astype(jnp.float32)
-                + high[:, s].astype(jnp.float32)
-            )
-            rows = slice((first + s) * PIECE, (first + s + 1) * PIECE)
-            out[:, rows] = total.astype(jnp.bfloat16)
-    lane = lax.broadcasted_iota(jnp.int32, (TAIL, LANES), 1)
-    labels = jnp.zeros((TAIL, LANES), jnp.int32)
-    for s in range(SLOTS):
-        labels = jnp.where(lane == s, owner[s] * OWN + local[s], labels)
-    labels = labels.astype(jnp.float32).astype(jnp.bfloat16)
-    out[:, SLOTS * PIECE :] = jnp.broadcast_to(labels[None], (N_DOM, TAIL, LANES))
-
-
-def finish(owner, local_id, parts):
-    return pl.pallas_call(
-        finish_kernel,
-        in_specs=[whole_smem()] * 2 + [whole_vmem()] * len(parts),
+def finish_kernel(first, count, *refs):
+    *labels, own, twin, low, high = refs[:-1] if first == 0 else refs[1:-1]
+    out = refs[-1]
+    for s in range(count):
+        total = (
+            own[0, :, s].astype(jnp.float32)
+            + twin[0, :, s].astype(jnp.float32)
+            + low[:, s].astype(jnp.float32)
+            + high[:, s].astype(jnp.float32)
+        )
+        rows = slice((first + s) * PIECE, (first + s + 1) * PIECE)
+        out[:, rows] = total.astype(jnp.bfloat16)
+    if labels:
+        owner, local = labels
+        lane = lax.broadcasted_iota(jnp.int32, (TAIL, LANES), 1)
+        tail = jnp.zeros((TAIL, LANES), jnp.int32)
+        for s in range(SLOTS):
+            tail = jnp.where(lane == s, owner[s] * OWN + local[s], tail)
+        tail = tail.astype(jnp.float32).astype(jnp.bfloat16)
+        out[:, SLOTS * PIECE :] = jnp.broadcast_to(tail[None], (N_DOM, TAIL, LANES))
+
+
+def finish(first, count, head, *parts):
+    return pl.pallas_call(
+        functools.partial(finish_kernel, first, count),
+        in_specs=([whole_vmem()] if first else [whole_smem()] * 2) + [whole_vmem()] * len(parts),
         out_specs=whole_vmem(),
         out_shape=jax.ShapeDtypeStruct((N_DOM, SLOTS * PIECE + TAIL, LANES), jnp.bfloat16),
+        input_output_aliases={0: 0} if first else {},
         compiler_params=pltpu.CompilerParams(vmem_limit_bytes=VMEM_LIMIT),
         name="finish",
-    )(owner, local_id, *parts)
+    )(*head, *parts)
 
 
 def sum_kernel(target, items, out, total):
@@ -160,14 +163,14 @@
 
 
 def on_device(solved, e_blocks, block_mask, owner, local_id):
-    solved = pltpu.with_memory_space_constraint(solved, pltpu.HBM)
+    pinned = pltpu.with_memory_space_constraint(solved, pltpu.HBM)
     e_blocks = pltpu.with_memory_space_constraint(e_blocks, pltpu.HBM)
     mask = pltpu.with_memory_space_constraint(block_mask.reshape(SLOTS), pltpu.HBM)
     sibling = [(g, g ^ 1) for g in range(N_GRP)]
     half = N_DOM // 2
-    parts = []
+    outgoing = None
     for first, count in CHUNKS:
-        own, other = product(solved, e_blocks, mask, first, count)
+        own, other = product(solved if first else pinned, e_blocks, mask, first, count)
         twin = lax.ppermute(other, "grp", sibling)
         far_up = total_of(own[2, :half], twin[2, :half])
         far_down = total_of(own[2, half:], twin[2, half:])
@@ -181,8 +184,9 @@
         )
         low = lax.ppermute(up, "grp", shift_z(1))
         high = lax.ppermute(down, "grp", shift_z(-1))
-        parts += [own, twin, low, high]
-    items = exchange(finish(owner.reshape(SLOTS), local_id.reshape(SLOTS), parts))
+        head = (outgoing,) if first else (owner.reshape(SLOTS), local_id.reshape(SLOTS))
+        outgoing = finish(first, count, head, own, twin, low, high)
+    items = exchange(outgoing)
     target = items[:, SLOTS * PIECE, :SLOTS].astype(jnp.int32)
     summed = sum_blocks(target.reshape(N_DOM * SLOTS), items)
     pieces = exchange(summed.reshape(N_DOM, OWN, PIECE, LANES))

time: 81.9 us -> 81 us (0.989)
    ppermute x2, waiting for transfers between devices: 11.5 us -> 10.7 us  [on_device(): low = lax.ppermute(up, 'grp', shift_z(1))]
  transfers between devices with their start and end apart: 10 -> 10, of which waited for: 3 -> 4; matrix products, arithmetic and copies ran while one was open for 1% -> 1% of each run, Pallas kernels for 6% -> 6%
where the time goes in v3:
time: 81 us; the launch traced here: 80.7 us
  blocking collectives  31.9 us (39%)
  waiting for transfers between devices  17.6 us (22%)
  Pallas kernels  15 us (19%)
  starting transfers between devices  14.8 us (18%)
  other arithmetic  1.15 us (1%)
    all_to_all x2, blocking collectives, exchange(): return lax.all_to_all(x, 'dom', split_axis=0, concat_axis=0, tiled=True)  31.9 us
    pallas_call x2, Pallas kernels, product(): pl.pallas_call(functools.partial(product_kernel, first), grid=(count,), i...  12.1 us
    ppermute x2, waiting for transfers between devices, on_device(): low = lax.ppermute(up, 'grp', shift_z(1))  10.7 us
    ppermute x2, starting transfers between devices, on_device(): from_above = lax.ppermute(far_down, 'grp', shift_z(-1))  7.54 us
    ppermute x2, starting transfers between devices, on_device(): high = lax.ppermute(down, 'grp', shift_z(-1))  6.57 us
    ppermute x2, waiting for transfers between devices, on_device(): from_below = lax.ppermute(far_up, 'grp', shift_z(1))  3.73 us
    ppermute x2, waiting for transfers between devices, on_device(): from_above = lax.ppermute(far_down, 'grp', shift_z(-1))  3.18 us
  transfers between devices with their start and end apart: 10, of which 4 were waited for; matrix products, arithmetic and copies ran while one was open for 1% of the time, Pallas kernels for 6%

profile of v3, /device:TPU:0, one launch (start us, length us, event | category | flops | bytes accessed | tf_op | source)
XLA Modules:
  0.0 80.7 jit_solution(10989086229056049258)
XLA Ops:
  0.0 0.0 copy-start
  0.0 7.7 %product.2 = (bf16[4,16,4,32,128]{4,3,2,1,0:T(8,128)(2,1)S(1)}, bf16[4,16,4,32,128]{4,3,2,1,0:T(8,128)(2,1)S(1)}) custom-call(s32[6]{0:T(128)} %bitcast.39, bf16[1,1024,512]{2,1,0:T(8,128)(2,1)} %factor.3, bf16[1,6,1024,1024]{3,2,1,0:T(8,128)(2,1)} %refs_3_.3, bf16[1,6,1024,1024]{3,2,1,0:T(8,128)(2,1)} %refs_3_.3, bf16[1,6,1024,1024]{3,2,1,0:T(8,128)(2,1)} %refs_3_.3, ...), custom_call_target="tpu_custom_call" | custom-call | tf_op jit(solution)/shard_map/product/pallas_call | solution.py:61
  7.7 0.1 collective-permute-start
  7.8 0.0 copy-done
  7.8 4.4 %product.3 = (bf16[4,16,2,32,128]{4,3,2,1,0:T(8,128)(2,1)S(1)}, bf16[4,16,2,32,128]{4,3,2,1,0:T(8,128)(2,1)S(1)}) custom-call(s32[6]{0:T(128)} %bitcast.40, bf16[1,1024,512]{2,1,0:T(8,128)(2,1)S(1)} %copy-done, bf16[1,6,1024,1024]{3,2,1,0:T(8,128)(2,1)} %refs_3_.3, bf16[1,6,1024,1024]{3,2,1,0:T(8,128)(2,1)} %refs_3_.3, bf16[1,6,1024,1024]{3,2,1,0:T(8,128)(2,1)} %refs_3_.3, ...), custom_call_target="tpu_custom_call" | custom-call | tf_op jit(solution)/shard_map/product/pallas_call | solution.py:61
  12.2 0.5 collective-permute-start.5
  12.7 0.0 collective-permute-done.refs_3_
  12.7 0.5 fusion.4
  13.1 4.2 %collective-permute-start.3 = (bf16[8,4,32,128]{3,2,1,0:T(8,128)(2,1)S(1)}, bf16[8,4,32,128]{3,2,1,0:T(8,128)(2,1)S(1)}, u32[]{:S(2)}, u32[]{:S(2)}) collective-permute-start(bf16[8,4,32,128]{3,2,1,0:T(8,128)(2,1)S(1)} %get-tuple-element.14), channel_id=1, source_target_pairs={{0,6},{1,7},{2,0},{3,1},{4,2},{5,3},{6,4},{7,5},{8,14},{9,15},{10,... | collective-permute-start | bytes 786440 | tf_op jit(solution)/shard_map/ppermute | solution.py:178
  17.4 0.0 collective-permute-start.1
  17.4 0.0 collective-permute-done.5.refs_2_
  17.4 0.2 fusion.10
  17.6 3.3 %collective-permute-start.8 = (bf16[8,2,32,128]{3,2,1,0:T(8,128)(2,1)S(1)}, bf16[8,2,32,128]{3,2,1,0:T(8,128)(2,1)S(1)}, u32[]{:S(2)}, u32[]{:S(2)}) collective-permute-start(bf16[8,2,32,128]{3,2,1,0:T(8,128)(2,1)S(1)} %get-tuple-element.20), channel_id=1, source_target_pairs={{0,6},{1,7},{2,0},{3,1},{4,2},{5,3},{6,4},{7,5},{8,14},{9,15},{10,... | collective-permute-start | bytes 393224 | tf_op jit(solution)/shard_map/ppermute | solution.py:178
  20.9 0.0 collective-permute-start.6
  20.9 3.2 %collective-permute-done.3 = bf16[8,4,32,128]{3,2,1,0:T(8,128)(2,1)S(1)} collective-permute-done((bf16[8,4,32,128]{3,2,1,0:T(8,128)(2,1)S(1)}, bf16[8,4,32,128]{3,2,1,0:T(8,128)(2,1)S(1)}, u32[]{:S(2)}, u32[]{:S(2)}) %collective-permute-start.3) | collective-permute-done | bytes 262176 | tf_op jit(solution)/shard_map/ppermute | solution.py:178
  24.1 3.7 %collective-permute-done.1 = bf16[8,4,32,128]{3,2,1,0:T(8,128)(2,1)S(1)} collective-permute-done((bf16[8,4,32,128]{3,2,1,0:T(8,128)(2,1)S(1)}, bf16[8,4,32,128]{3,2,1,0:T(8,128)(2,1)S(1)}, u32[]{:S(2)}, u32[]{:S(2)}) %collective-permute-start.1) | collective-permute-done | bytes 262176 | tf_op jit(solution)/shard_map/ppermute | solution.py:177
  27.8 0.2 fusion
  28.0 0.0 copy-start.1
  28.0 0.0 copy-start.2
  28.1 0.1 collective-permute-start.2
  28.2 3.3 %collective-permute-start.4 = (bf16[16,4,32,128]{3,2,1,0:T(8,128)(2,1)S(1)}, bf16[16,4,32,128]{3,2,1,0:T(8,128)(2,1)S(1)}, u32[]{:S(2)}, u32[]{:S(2)}) collective-permute-start(bf16[16,4,32,128]{3,2,1,0:T(8,128)(2,1)S(1)} %pad_maximum_fusion.1), channel_id=1, source_target_pairs={{0,6},{1,7},{2,0},{3,1},{4,2},{5,3},{6,4},{7,5},{8,14},{9,15},{10,... | collective-permute-start | bytes 1572872 | tf_op jit(solution)/shard_map/ppermute | solution.py:186
  31.5 0.0 collective-permute-done.8
  31.5 0.0 collective-permute-done.6
  31.5 0.1 fusion.6
  31.7 0.1 collective-permute-start.7
  31.8 3.3 %collective-permute-start.9 = (bf16[16,2,32,128]{3,2,1,0:T(8,128)(2,1)S(1)}, bf16[16,2,32,128]{3,2,1,0:T(8,128)(2,1)S(1)}, u32[]{:S(2)}, u32[]{:S(2)}) collective-permute-start(bf16[16,2,32,128]{3,2,1,0:T(8,128)(2,1)S(1)} %pad_maximum_fusion.3), channel_id=1, source_target_pairs={{0,6},{1,7},{2,0},{3,1},{4,2},{5,3},{6,4},{7,5},{8,14},{9,15},{10,... | collective-permute-start | bytes 786440 | tf_op jit(solution)/shard_map/ppermute | solution.py:186
  35.1 8.7 %collective-permute-done.2.refs_4_ = bf16[16,4,32,128]{3,2,1,0:T(8,128)(2,1)S(1)} collective-permute-done((bf16[16,4,32,128]{3,2,1,0:T(8,128)(2,1)S(1)}, bf16[16,4,32,128]{3,2,1,0:T(8,128)(2,1)S(1)}, u32[]{:S(2)}, u32[]{:S(2)}) %collective-permute-start.2) | collective-permute-done | bytes 524320 | tf_op jit(solution)/shard_map/ppermute | solution.py:185
  43.8 0.0 collective-permute-done.4.refs_5_
  43.8 0.0 copy-done.1
  43.8 0.0 copy-done.2
  43.8 0.8 %finish.2.refs_0_ = bf16[16,200,128]{2,1,0:T(8,128)(2,1)S(1)} custom-call(s32[6]{0:T(128)S(1)} %bitcast.37, s32[6]{0:T(128)S(1)} %bitcast.38, bf16[4,16,4,32,128]{4,3,2,1,0:T(8,128)(2,1)S(1)} %get-tuple-element.9.refs_2_, bf16[4,16,4,32,128]{4,3,2,1,0:T(8,128)(2,1)S(1)} %collective-permute-done.refs_3_, ...), custom_call_target="tpu_custom_call" | custom-call | tf_op jit(solution)/shard_map/finish/pallas_call | solution.py:96
  44.6 2.0 %collective-permute-done.7.refs_3_ = bf16[16,2,32,128]{3,2,1,0:T(8,128)(2,1)S(1)} collective-permute-done((bf16[16,2,32,128]{3,2,1,0:T(8,128)(2,1)S(1)}, bf16[16,2,32,128]{3,2,1,0:T(8,128)(2,1)S(1)}, u32[]{:S(2)}, u32[]{:S(2)}) %collective-permute-start.7) | collective-permute-done | bytes 262176 | tf_op jit(solution)/shard_map/ppermute | solution.py:185
  46.6 0.0 collective-permute-done.9.refs_4_
  46.6 0.1 finish.3
  46.7 18.3 %all_to_all.10.items = bf16[16,200,128]{2,1,0:T(8,128)(2,1)S(1)} all-to-all(bf16[16,200,128]{2,1,0:T(8,128)(2,1)S(1)} %finish.3), channel_id=1, replica_groups=mesh['dom'=16,'grp'=8] {'dom'}, dimensions={0} | all-to-all | bytes 1638400 | tf_op jit(solution)/shard_map/all_to_all | solution.py:162
  65.1 0.1 reshape.64.target
  65.2 1.0 %sum_blocks.1 = bf16[64,32,128]{2,1,0:T(8,128)(2,1)S(1)} custom-call(s32[96]{0:T(128)S(1)} %reshape.64.target, bf16[16,200,128]{2,1,0:T(8,128)(2,1)S(1)} %all_to_all.10.items), custom_call_target="tpu_custom_call" | custom-call | tf_op jit(solution)/shard_map/sum_blocks/pallas_call | solution.py:123
  66.2 13.5 %all_to_all.11.pieces = bf16[16,4,32,128]{3,2,1,0:T(8,128)(2,1)S(1)} all-to-all(bf16[16,4,32,128]{3,2,1,0:T(8,128)(2,1)S(1)} %bitcast.36), channel_id=1, replica_groups=mesh['dom'=16,'grp'=8] {'dom'}, dimensions={0} | all-to-all | bytes 1048576 | tf_op jit(solution)/shard_map/all_to_all | solution.py:162
  79.7 1.0 %turn_back.1 = bf16[4,128,512]{2,1,0:T(8,128)(2,1)} custom-call(bf16[16,4,32,128]{3,2,1,0:T(8,128)(2,1)S(1)} %all_to_all.11.pieces), custom_call_target="tpu_custom_call" | custom-call | tf_op jit(solution)/shard_map/turn_back/pallas_call | solution.py:140
  (5 shorter events, 0.2 us)
Async XLA Ops:
  0.0 7.8 %copy-start = (bf16[1,1024,512]{2,1,0:T(8,128)(2,1)S(1)}, bf16[1,1024,512]{2,1,0:T(8,128)(2,1)}, u32[]{:S(2)}) copy-start(bf16[1,1024,512]{2,1,0:T(8,128)(2,1)} %factor.3) | copy-start | bytes 3145732
  7.7 5.0 %collective-permute-start = (bf16[4,16,4,32,128]{4,3,2,1,0:T(8,128)(2,1)S(1)}, bf16[4,16,4,32,128]{4,3,2,1,0:T(8,128)(2,1)S(1)}, u32[]{:S(2)}, u32[]{:S(2)}) collective-permute-start(bf16[4,16,4,32,128]{4,3,2,1,0:T(8,128)(2,1)S(1)} %get-tuple-element.10), channel_id=1, source_target_pairs={{0,1},{1,0},{2,3},{3,2},{4,5},{5,4},{6,7},{7,6},{8,9},{9,8},{10,11... | collective-permute-start | bytes 6291464 | tf_op jit(solution)/shard_map/ppermute | solution.py:174
  12.2 5.2 %collective-permute-start.5 = (bf16[4,16,2,32,128]{4,3,2,1,0:T(8,128)(2,1)S(1)}, bf16[4,16,2,32,128]{4,3,2,1,0:T(8,128)(2,1)S(1)}, u32[]{:S(2)}, u32[]{:S(2)}) collective-permute-start(bf16[4,16,2,32,128]{4,3,2,1,0:T(8,128)(2,1)S(1)} %get-tuple-element.12), channel_id=1, source_target_pairs={{0,1},{1,0},{2,3},{3,2},{4,5},{5,4},{6,7},{7,6},{8,9},{9,8},{10,11... | collective-permute-start | bytes 3145736 | tf_op jit(solution)/shard_map/ppermute | solution.py:174
  13.1 10.9 %collective-permute-start.3 = (bf16[8,4,32,128]{3,2,1,0:T(8,128)(2,1)S(1)}, bf16[8,4,32,128]{3,2,1,0:T(8,128)(2,1)S(1)}, u32[]{:S(2)}, u32[]{:S(2)}) collective-permute-start(bf16[8,4,32,128]{3,2,1,0:T(8,128)(2,1)S(1)} %get-tuple-element.14), channel_id=1, source_target_pairs={{0,6},{1,7},{2,0},{3,1},{4,2},{5,3},{6,4},{7,5},{8,14},{9,15},{10,... | collective-permute-start | bytes 786440 | tf_op jit(solution)/shard_map/ppermute | solution.py:178
  17.4 10.4 %collective-permute-start.1 = (bf16[8,4,32,128]{3,2,1,0:T(8,128)(2,1)S(1)}, bf16[8,4,32,128]{3,2,1,0:T(8,128)(2,1)S(1)}, u32[]{:S(2)}, u32[]{:S(2)}) collective-permute-start(bf16[8,4,32,128]{3,2,1,0:T(8,128)(2,1)S(1)} %get-tuple-element.16), channel_id=1, source_target_pairs={{0,2},{1,3},{2,4},{3,5},{4,6},{5,7},{6,0},{7,1},{8,10},{9,11},{10,... | collective-permute-start | bytes 786440 | tf_op jit(solution)/shard_map/ppermute | solution.py:177
  17.6 14.0 %collective-permute-start.8 = (bf16[8,2,32,128]{3,2,1,0:T(8,128)(2,1)S(1)}, bf16[8,2,32,128]{3,2,1,0:T(8,128)(2,1)S(1)}, u32[]{:S(2)}, u32[]{:S(2)}) collective-permute-start(bf16[8,2,32,128]{3,2,1,0:T(8,128)(2,1)S(1)} %get-tuple-element.20), channel_id=1, source_target_pairs={{0,6},{1,7},{2,0},{3,1},{4,2},{5,3},{6,4},{7,5},{8,14},{9,15},{10,... | collective-permute-start | bytes 393224 | tf_op jit(solution)/shard_map/ppermute | solution.py:178
  20.9 10.7 %collective-permute-start.6 = (bf16[8,2,32,128]{3,2,1,0:T(8,128)(2,1)S(1)}, bf16[8,2,32,128]{3,2,1,0:T(8,128)(2,1)S(1)}, u32[]{:S(2)}, u32[]{:S(2)}) collective-permute-start(bf16[8,2,32,128]{3,2,1,0:T(8,128)(2,1)S(1)} %get-tuple-element.22), channel_id=1, source_target_pairs={{0,2},{1,3},{2,4},{3,5},{4,6},{5,7},{6,0},{7,1},{8,10},{9,11},{10,... | collective-permute-start | bytes 393224 | tf_op jit(solution)/shard_map/ppermute | solution.py:177
  28.0 15.8 %copy-start.1 = (s32[1,6,1]{1,2,0:T(1,128)S(1)}, s32[1,6,1]{1,2,0:T(1,128)}, u32[]{:S(2)}) copy-start(s32[1,6,1]{1,2,0:T(1,128)} %param.8) | copy-start | bytes 76
  28.0 15.7 %copy-start.2 = (s32[1,6]{1,0:T(1,128)S(1)}, s32[1,6]{1,0:T(1,128)}, u32[]{:S(2)}) copy-start(s32[1,6]{1,0:T(1,128)} %param.9) | copy-start | bytes 76
  28.1 15.7 %collective-permute-start.2 = (bf16[16,4,32,128]{3,2,1,0:T(8,128)(2,1)S(1)}, bf16[16,4,32,128]{3,2,1,0:T(8,128)(2,1)S(1)}, u32[]{:S(2)}, u32[]{:S(2)}) collective-permute-start(bf16[16,4,32,128]{3,2,1,0:T(8,128)(2,1)S(1)} %pad_maximum_fusion), channel_id=1, source_target_pairs={{0,2},{1,3},{2,4},{3,5},{4,6},{5,7},{6,0},{7,1},{8,10},{9,11},{10,... | collective-permute-start | bytes 1572872 | tf_op jit(solution)/shard_map/ppermute | solution.py:185
  28.2 15.5 %collective-permute-start.4 = (bf16[16,4,32,128]{3,2,1,0:T(8,128)(2,1)S(1)}, bf16[16,4,32,128]{3,2,1,0:T(8,128)(2,1)S(1)}, u32[]{:S(2)}, u32[]{:S(2)}) collective-permute-start(bf16[16,4,32,128]{3,2,1,0:T(8,128)(2,1)S(1)} %pad_maximum_fusion.1), channel_id=1, source_target_pairs={{0,6},{1,7},{2,0},{3,1},{4,2},{5,3},{6,4},{7,5},{8,14},{9,15},{10,... | collective-permute-start | bytes 1572872 | tf_op jit(solution)/shard_map/ppermute | solution.py:186
  31.7 14.9 %collective-permute-start.7 = (bf16[16,2,32,128]{3,2,1,0:T(8,128)(2,1)S(1)}, bf16[16,2,32,128]{3,2,1,0:T(8,128)(2,1)S(1)}, u32[]{:S(2)}, u32[]{:S(2)}) collective-permute-start(bf16[16,2,32,128]{3,2,1,0:T(8,128)(2,1)S(1)} %pad_maximum_fusion.2), channel_id=1, source_target_pairs={{0,2},{1,3},{2,4},{3,5},{4,6},{5,7},{6,0},{7,1},{8,10},{9,11},{10,... | collective-permute-start | bytes 786440 | tf_op jit(solution)/shard_map/ppermute | solution.py:185
  31.8 14.8 %collective-permute-start.9 = (bf16[16,2,32,128]{3,2,1,0:T(8,128)(2,1)S(1)}, bf16[16,2,32,128]{3,2,1,0:T(8,128)(2,1)S(1)}, u32[]{:S(2)}, u32[]{:S(2)}) collective-permute-start(bf16[16,2,32,128]{3,2,1,0:T(8,128)(2,1)S(1)} %pad_maximum_fusion.3), channel_id=1, source_target_pairs={{0,6},{1,7},{2,0},{3,1},{4,2},{5,3},{6,4},{7,5},{8,14},{9,15},{10,... | collective-permute-start | bytes 786440 | tf_op jit(solution)/shard_map/ppermute | solution.py:186

commit v4 on v3

--- a/solution.py
+++ b/solution.py
@@ -16,7 +16,7 @@
 LANES = BLK // N_GRP
 PIECE = COLS // N_DOM
 TAIL = 8
-CHUNKS = ((0, 4), (4, 2))
+CHUNKS = ((0, 3), (3, 3))
 CONTRACT_ROWS = (((0,), (0,)), ((), ()))
 VMEM_LIMIT = 24 << 20
 
@@ -71,17 +71,19 @@
 
 
 def finish_kernel(first, count, *refs):
-    *labels, own, twin, low, high = refs[:-1] if first == 0 else refs[1:-1]
+    *labels, own, twin, below, above, low, high = refs[:-1] if first == 0 else refs[1:-1]
     out = refs[-1]
+    half = N_DOM // 2
     for s in range(count):
-        total = (
-            own[0, :, s].astype(jnp.float32)
-            + twin[0, :, s].astype(jnp.float32)
-            + low[:, s].astype(jnp.float32)
-            + high[:, s].astype(jnp.float32)
-        )
         rows = slice((first + s) * PIECE, (first + s + 1) * PIECE)
-        out[:, rows] = total.astype(jnp.bfloat16)
+        for here, ring in (
+            (slice(0, half), (above[half:, s], low[:, s])),
+            (slice(half, N_DOM), (below[:half, s], high[:, s])),
+        ):
+            total = own[0, here, s].astype(jnp.float32) + twin[0, here, s].astype(jnp.float32)
+            for term in ring:
+                total = total + term.astype(jnp.float32)
+            out[here, rows] = total.astype(jnp.bfloat16)
     if labels:
         owner, local = labels
         lane = lax.broadcasted_iota(jnp.int32, (TAIL, LANES), 1)
@@ -172,20 +174,18 @@
     for first, count in CHUNKS:
         own, other = product(solved if first else pinned, e_blocks, mask, first, count)
         twin = lax.ppermute(other, "grp", sibling)
-        far_up = total_of(own[2, :half], twin[2, :half])
-        far_down = total_of(own[2, half:], twin[2, half:])
-        from_below = lax.ppermute(far_up, "grp", shift_z(1))
-        from_above = lax.ppermute(far_down, "grp", shift_z(-1))
-        up = jnp.concatenate(
-            [total_of(own[1, :half], twin[1, :half], from_below), total_of(own[1, half:], twin[1, half:])]
-        )
-        down = jnp.concatenate(
-            [total_of(own[3, :half], twin[3, :half]), total_of(own[3, half:], twin[3, half:], from_above)]
-        )
-        low = lax.ppermute(up, "grp", shift_z(1))
-        high = lax.ppermute(down, "grp", shift_z(-1))
+        flat = (N_Z * N_DOM, count, PIECE, LANES)
+        mine, yours = own.reshape(flat), twin.reshape(flat)
+
+        def both(start, stop, *more):
+            return total_of(mine[start:stop], yours[start:stop], *more)
+
+        below = lax.ppermute(both(3 * half, 5 * half), "grp", shift_z(1))
+        above = lax.ppermute(both(5 * half, 7 * half), "grp", shift_z(-1))
+        low = lax.ppermute(both(2 * half, 3 * half, below[half:]), "grp", shift_z(1))
+        high = lax.ppermute(both(7 * half, 8 * half, above[:half]), "grp", shift_z(-1))
         head = (outgoing,) if first else (owner.reshape(SLOTS), local_id.reshape(SLOTS))
-        outgoing = finish(first, count, head, own, twin, low, high)
+        outgoing = finish(first, count, head, own, twin, below, above, low, high)
     items = exchange(outgoing)
     target = items[:, SLOTS * PIECE, :SLOTS].astype(jnp.int32)
     summed = sum_blocks(target.reshape(N_DOM * SLOTS), items)

time: 81 us -> 79.6 us (0.983)
  waiting for transfers between devices: 17.6 us -> 14.5 us
  blocking collectives: 31.9 us -> 33.6 us
    ppermute x8, waiting for transfers between devices: 17.6 us -> 14.5 us  [the longest x2 11.1 us: on_device(): below = lax.ppermute(both(3 * half, 5 * half), 'grp', shift_z(1))]
    all_to_all x2, blocking collectives: 31.9 us -> 33.6 us  [exchange(): return lax.all_to_all(x, 'dom', split_axis=0, concat_axis=0, tiled=True)]
  transfers between devices with their start and end apart: 10 -> 10, of which waited for: 4 -> 4; matrix products, arithmetic and copies ran while one was open for 1% -> 1% of each run, Pallas kernels for 6% -> 8%
where the time goes in v4:
time: 79.6 us; the launch traced here: 79.4 us
  blocking collectives  33.6 us (42%)
  starting transfers between devices  15.2 us (19%)
  Pallas kernels  15.1 us (19%)
  waiting for transfers between devices  14.5 us (18%)
    all_to_all x2, blocking collectives, exchange(): return lax.all_to_all(x, 'dom', split_axis=0, concat_axis=0, tiled=True)  33.6 us
    pallas_call x2, Pallas kernels, product(): pl.pallas_call(functools.partial(product_kernel, first), grid=(count,), i...  12.2 us
    ppermute x2, waiting for transfers between devices, on_device(): below = lax.ppermute(both(3 * half, 5 * half), 'grp', shift_z(1))  11.1 us
    ppermute x2, starting transfers between devices, on_device(): above = lax.ppermute(both(5 * half, 7 * half), 'grp', shift_z(-1))  4.87 us
    ppermute x2, starting transfers between devices, on_device(): lax.ppermute(both(2 * half, 3 * half, below[half:]), 'grp', shift_z(1))  3.93 us
    ppermute x2, waiting for transfers between devices, on_device(): lax.ppermute(both(2 * half, 3 * half, below[half:]), 'grp', shift_z(1))  3.45 us
    ppermute x2, starting transfers between devices, on_device(): lax.ppermute(both(7 * half, 8 * half, above[:half]), 'grp', shift_z(-1))  3.07 us
    ppermute x2, starting transfers between devices, on_device(): below = lax.ppermute(both(3 * half, 5 * half), 'grp', shift_z(1))  2.75 us
  transfers between devices with their start and end apart: 10, of which 4 were waited for; matrix products, arithmetic and copies ran while one was open for 1% of the time, Pallas kernels for 8%

profile of v4, /device:TPU:0, one launch (start us, length us, event | category | flops | bytes accessed | tf_op | source)
XLA Modules:
  0.0 79.4 jit_solution(9558205438005459862)
XLA Ops:
  0.0 0.0 copy-start
  0.0 6.3 %product.2 = (bf16[4,16,3,32,128]{4,3,2,1,0:T(8,128)(2,1)S(1)}, bf16[4,16,3,32,128]{4,3,2,1,0:T(8,128)(2,1)S(1)}) custom-call(s32[6]{0:T(128)} %bitcast.19, bf16[1,1024,512]{2,1,0:T(8,128)(2,1)} %factor.3, bf16[1,6,1024,1024]{3,2,1,0:T(8,128)(2,1)} %refs_3_.3, bf16[1,6,1024,1024]{3,2,1,0:T(8,128)(2,1)} %refs_3_.3, bf16[1,6,1024,1024]{3,2,1,0:T(8,128)(2,1)} %refs_3_.3, ...), custom_call_target="tpu_custom_call" | custom-call | tf_op jit(solution)/shard_map/product/pallas_call | solution.py:61
  6.3 0.1 collective-permute-start
  6.4 0.0 copy-done
  6.4 5.9 %product.3 = (bf16[4,16,3,32,128]{4,3,2,1,0:T(8,128)(2,1)S(1)}, bf16[4,16,3,32,128]{4,3,2,1,0:T(8,128)(2,1)S(1)}) custom-call(s32[6]{0:T(128)} %bitcast.20, bf16[1,1024,512]{2,1,0:T(8,128)(2,1)S(1)} %copy-done, bf16[1,6,1024,1024]{3,2,1,0:T(8,128)(2,1)} %refs_3_.3, bf16[1,6,1024,1024]{3,2,1,0:T(8,128)(2,1)} %refs_3_.3, bf16[1,6,1024,1024]{3,2,1,0:T(8,128)(2,1)} %refs_3_.3, ...), custom_call_target="tpu_custom_call" | custom-call | tf_op jit(solution)/shard_map/product/pallas_call | solution.py:61
  12.3 0.5 collective-permute-start.5
  12.8 0.0 collective-permute-done.refs_3_
  12.8 0.2 add_convert_fusion.2
  13.0 2.1 %collective-permute-start.1 = (bf16[16,3,32,128]{3,2,1,0:T(8,128)(2,1)S(1)}, bf16[16,3,32,128]{3,2,1,0:T(8,128)(2,1)S(1)}, u32[]{:S(2)}, u32[]{:S(2)}) collective-permute-start(bf16[16,3,32,128]{3,2,1,0:T(8,128)(2,1)S(1)} %get-tuple-element.20), channel_id=1, source_target_pairs={{0,2},{1,3},{2,4},{3,5},{4,6},{5,7},{6,0},{7,1},{8,10},{9,11},{10,... | collective-permute-start | bytes 1179656 | tf_op jit(solution)/shard_map/ppermute | solution.py:183
  15.1 2.2 %collective-permute-start.2 = (bf16[16,3,32,128]{3,2,1,0:T(8,128)(2,1)S(1)}, bf16[16,3,32,128]{3,2,1,0:T(8,128)(2,1)S(1)}, u32[]{:S(2)}, u32[]{:S(2)}) collective-permute-start(bf16[16,3,32,128]{3,2,1,0:T(8,128)(2,1)S(1)} %get-tuple-element.19), channel_id=1, source_target_pairs={{0,6},{1,7},{2,0},{3,1},{4,2},{5,3},{6,4},{7,5},{8,14},{9,15},{10,... | collective-permute-start | bytes 1179656 | tf_op jit(solution)/shard_map/ppermute | solution.py:184
  17.3 0.0 collective-permute-done.5.refs_2_
  17.3 0.2 add_convert_fusion
  17.5 0.6 collective-permute-start.6
  18.2 0.0 copy-start.1
  18.2 0.0 copy-start.2
  18.2 2.7 %collective-permute-start.7 = (bf16[16,3,32,128]{3,2,1,0:T(8,128)(2,1)S(1)}, bf16[16,3,32,128]{3,2,1,0:T(8,128)(2,1)S(1)}, u32[]{:S(2)}, u32[]{:S(2)}) collective-permute-start(bf16[16,3,32,128]{3,2,1,0:T(8,128)(2,1)S(1)} %get-tuple-element.15), channel_id=1, source_target_pairs={{0,6},{1,7},{2,0},{3,1},{4,2},{5,3},{6,4},{7,5},{8,14},{9,15},{10,... | collective-permute-start | bytes 1179656 | tf_op jit(solution)/shard_map/ppermute | solution.py:184
  20.8 6.3 %collective-permute-done.1.refs_4_ = bf16[16,3,32,128]{3,2,1,0:T(8,128)(2,1)S(1)} collective-permute-done((bf16[16,3,32,128]{3,2,1,0:T(8,128)(2,1)S(1)}, bf16[16,3,32,128]{3,2,1,0:T(8,128)(2,1)S(1)}, u32[]{:S(2)}, u32[]{:S(2)}) %collective-permute-start.1) | collective-permute-done | bytes 393248 | tf_op jit(solution)/shard_map/ppermute | solution.py:183
  27.1 0.0 collective-permute-done.2.refs_5_
  27.1 0.2 add_convert_fusion.6
  27.3 2.0 %collective-permute-start.3 = (bf16[8,3,32,128]{3,2,1,0:T(8,128)(2,1)S(1)}, bf16[8,3,32,128]{3,2,1,0:T(8,128)(2,1)S(1)}, u32[]{:S(2)}, u32[]{:S(2)}) collective-permute-start(bf16[8,3,32,128]{3,2,1,0:T(8,128)(2,1)S(1)} %get-tuple-element.18), channel_id=1, source_target_pairs={{0,2},{1,3},{2,4},{3,5},{4,6},{5,7},{6,0},{7,1},{8,10},{9,11},{10,... | collective-permute-start | bytes 589832 | tf_op jit(solution)/shard_map/ppermute | solution.py:185
  29.3 1.5 %collective-permute-start.4 = (bf16[8,3,32,128]{3,2,1,0:T(8,128)(2,1)S(1)}, bf16[8,3,32,128]{3,2,1,0:T(8,128)(2,1)S(1)}, u32[]{:S(2)}, u32[]{:S(2)}) collective-permute-start(bf16[8,3,32,128]{3,2,1,0:T(8,128)(2,1)S(1)} %get-tuple-element.17), channel_id=1, source_target_pairs={{0,6},{1,7},{2,0},{3,1},{4,2},{5,3},{6,4},{7,5},{8,14},{9,15},{10,... | collective-permute-start | bytes 589832 | tf_op jit(solution)/shard_map/ppermute | solution.py:186
  30.8 4.8 %collective-permute-done.6.refs_3_ = bf16[16,3,32,128]{3,2,1,0:T(8,128)(2,1)S(1)} collective-permute-done((bf16[16,3,32,128]{3,2,1,0:T(8,128)(2,1)S(1)}, bf16[16,3,32,128]{3,2,1,0:T(8,128)(2,1)S(1)}, u32[]{:S(2)}, u32[]{:S(2)}) %collective-permute-start.6) | collective-permute-done | bytes 393248 | tf_op jit(solution)/shard_map/ppermute | solution.py:183
  35.6 0.0 collective-permute-done.7.refs_4_
  35.6 0.2 add_convert_fusion.4
  35.7 2.0 %collective-permute-start.8 = (bf16[8,3,32,128]{3,2,1,0:T(8,128)(2,1)S(1)}, bf16[8,3,32,128]{3,2,1,0:T(8,128)(2,1)S(1)}, u32[]{:S(2)}, u32[]{:S(2)}) collective-permute-start(bf16[8,3,32,128]{3,2,1,0:T(8,128)(2,1)S(1)} %get-tuple-element.14), channel_id=1, source_target_pairs={{0,2},{1,3},{2,4},{3,5},{4,6},{5,7},{6,0},{7,1},{8,10},{9,11},{10,... | collective-permute-start | bytes 589832 | tf_op jit(solution)/shard_map/ppermute | solution.py:185
  37.7 1.5 %collective-permute-start.9 = (bf16[8,3,32,128]{3,2,1,0:T(8,128)(2,1)S(1)}, bf16[8,3,32,128]{3,2,1,0:T(8,128)(2,1)S(1)}, u32[]{:S(2)}, u32[]{:S(2)}) collective-permute-start(bf16[8,3,32,128]{3,2,1,0:T(8,128)(2,1)S(1)} %get-tuple-element.13), channel_id=1, source_target_pairs={{0,6},{1,7},{2,0},{3,1},{4,2},{5,3},{6,4},{7,5},{8,14},{9,15},{10,... | collective-permute-start | bytes 589832 | tf_op jit(solution)/shard_map/ppermute | solution.py:186
  39.2 0.5 collective-permute-done.3.refs_6_
  39.8 0.0 collective-permute-done.4.refs_7_
  39.8 0.0 copy-done.1
  39.8 0.0 copy-done.2
  39.8 0.8 finish.2.refs_0_
  40.5 2.9 %collective-permute-done.8.refs_5_ = bf16[8,3,32,128]{3,2,1,0:T(8,128)(2,1)S(1)} collective-permute-done((bf16[8,3,32,128]{3,2,1,0:T(8,128)(2,1)S(1)}, bf16[8,3,32,128]{3,2,1,0:T(8,128)(2,1)S(1)}, u32[]{:S(2)}, u32[]{:S(2)}) %collective-permute-start.8) | collective-permute-done | bytes 196640 | tf_op jit(solution)/shard_map/ppermute | solution.py:185
  43.4 0.0 collective-permute-done.9.refs_6_
  43.5 0.2 finish.3
  43.7 20.0 %all_to_all.10.items = bf16[16,200,128]{2,1,0:T(8,128)(2,1)S(1)} all-to-all(bf16[16,200,128]{2,1,0:T(8,128)(2,1)S(1)} %finish.3), channel_id=1, replica_groups=mesh['dom'=16,'grp'=8] {'dom'}, dimensions={0} | all-to-all | bytes 1638400 | tf_op jit(solution)/shard_map/all_to_all | solution.py:164
  63.7 0.1 reshape.36.target
  63.8 1.0 %sum_blocks.1 = bf16[64,32,128]{2,1,0:T(8,128)(2,1)S(1)} custom-call(s32[96]{0:T(128)S(1)} %reshape.36.target, bf16[16,200,128]{2,1,0:T(8,128)(2,1)S(1)} %all_to_all.10.items), custom_call_target="tpu_custom_call" | custom-call | tf_op jit(solution)/shard_map/sum_blocks/pallas_call | solution.py:125
  64.9 13.5 %all_to_all.11.pieces = bf16[16,4,32,128]{3,2,1,0:T(8,128)(2,1)S(1)} all-to-all(bf16[16,4,32,128]{3,2,1,0:T(8,128)(2,1)S(1)} %bitcast.16), channel_id=1, replica_groups=mesh['dom'=16,'grp'=8] {'dom'}, dimensions={0} | all-to-all | bytes 1048576 | tf_op jit(solution)/shard_map/all_to_all | solution.py:164
  78.4 1.0 %turn_back.1 = bf16[4,128,512]{2,1,0:T(8,128)(2,1)} custom-call(bf16[16,4,32,128]{3,2,1,0:T(8,128)(2,1)S(1)} %all_to_all.11.pieces), custom_call_target="tpu_custom_call" | custom-call | tf_op jit(solution)/shard_map/turn_back/pallas_call | solution.py:142
  (1 shorter events, 0.0 us)
Async XLA Ops:
  0.0 6.4 %copy-start = (bf16[1,1024,512]{2,1,0:T(8,128)(2,1)S(1)}, bf16[1,1024,512]{2,1,0:T(8,128)(2,1)}, u32[]{:S(2)}) copy-start(bf16[1,1024,512]{2,1,0:T(8,128)(2,1)} %factor.3) | copy-start | bytes 3145732
  6.3 6.5 %collective-permute-start = (bf16[4,16,3,32,128]{4,3,2,1,0:T(8,128)(2,1)S(1)}, bf16[4,16,3,32,128]{4,3,2,1,0:T(8,128)(2,1)S(1)}, u32[]{:S(2)}, u32[]{:S(2)}) collective-permute-start(bf16[4,16,3,32,128]{4,3,2,1,0:T(8,128)(2,1)S(1)} %get-tuple-element.10), channel_id=1, source_target_pairs={{0,1},{1,0},{2,3},{3,2},{4,5},{5,4},{6,7},{7,6},{8,9},{9,8},{10,11... | collective-permute-start | bytes 4718600 | tf_op jit(solution)/shard_map/ppermute | solution.py:176
  12.3 5.0 %collective-permute-start.5 = (bf16[4,16,3,32,128]{4,3,2,1,0:T(8,128)(2,1)S(1)}, bf16[4,16,3,32,128]{4,3,2,1,0:T(8,128)(2,1)S(1)}, u32[]{:S(2)}, u32[]{:S(2)}) collective-permute-start(bf16[4,16,3,32,128]{4,3,2,1,0:T(8,128)(2,1)S(1)} %get-tuple-element.12), channel_id=1, source_target_pairs={{0,1},{1,0},{2,3},{3,2},{4,5},{5,4},{6,7},{7,6},{8,9},{9,8},{10,11... | collective-permute-start | bytes 4718600 | tf_op jit(solution)/shard_map/ppermute | solution.py:176
  13.0 14.1 %collective-permute-start.1 = (bf16[16,3,32,128]{3,2,1,0:T(8,128)(2,1)S(1)}, bf16[16,3,32,128]{3,2,1,0:T(8,128)(2,1)S(1)}, u32[]{:S(2)}, u32[]{:S(2)}) collective-permute-start(bf16[16,3,32,128]{3,2,1,0:T(8,128)(2,1)S(1)} %get-tuple-element.20), channel_id=1, source_target_pairs={{0,2},{1,3},{2,4},{3,5},{4,6},{5,7},{6,0},{7,1},{8,10},{9,11},{10,... | collective-permute-start | bytes 1179656 | tf_op jit(solution)/shard_map/ppermute | solution.py:183
  15.1 12.0 %collective-permute-start.2 = (bf16[16,3,32,128]{3,2,1,0:T(8,128)(2,1)S(1)}, bf16[16,3,32,128]{3,2,1,0:T(8,128)(2,1)S(1)}, u32[]{:S(2)}, u32[]{:S(2)}) collective-permute-start(bf16[16,3,32,128]{3,2,1,0:T(8,128)(2,1)S(1)} %get-tuple-element.19), channel_id=1, source_target_pairs={{0,6},{1,7},{2,0},{3,1},{4,2},{5,3},{6,4},{7,5},{8,14},{9,15},{10,... | collective-permute-start | bytes 1179656 | tf_op jit(solution)/shard_map/ppermute | solution.py:184
  17.5 18.0 %collective-permute-start.6 = (bf16[16,3,32,128]{3,2,1,0:T(8,128)(2,1)S(1)}, bf16[16,3,32,128]{3,2,1,0:T(8,128)(2,1)S(1)}, u32[]{:S(2)}, u32[]{:S(2)}) collective-permute-start(bf16[16,3,32,128]{3,2,1,0:T(8,128)(2,1)S(1)} %get-tuple-element.16), channel_id=1, source_target_pairs={{0,2},{1,3},{2,4},{3,5},{4,6},{5,7},{6,0},{7,1},{8,10},{9,11},{10,... | collective-permute-start | bytes 1179656 | tf_op jit(solution)/shard_map/ppermute | solution.py:183
  18.2 21.6 %copy-start.1 = (s32[1,6,1]{1,2,0:T(1,128)S(1)}, s32[1,6,1]{1,2,0:T(1,128)}, u32[]{:S(2)}) copy-start(s32[1,6,1]{1,2,0:T(1,128)} %param.8) | copy-start | bytes 76
  18.2 21.6 %copy-start.2 = (s32[1,6]{1,0:T(1,128)S(1)}, s32[1,6]{1,0:T(1,128)}, u32[]{:S(2)}) copy-start(s32[1,6]{1,0:T(1,128)} %param.9) | copy-start | bytes 76
  18.2 17.4 %collective-permute-start.7 = (bf16[16,3,32,128]{3,2,1,0:T(8,128)(2,1)S(1)}, bf16[16,3,32,128]{3,2,1,0:T(8,128)(2,1)S(1)}, u32[]{:S(2)}, u32[]{:S(2)}) collective-permute-start(bf16[16,3,32,128]{3,2,1,0:T(8,128)(2,1)S(1)} %get-tuple-element.15), channel_id=1, source_target_pairs={{0,6},{1,7},{2,0},{3,1},{4,2},{5,3},{6,4},{7,5},{8,14},{9,15},{10,... | collective-permute-start | bytes 1179656 | tf_op jit(solution)/shard_map/ppermute | solution.py:184
  27.3 12.5 %collective-permute-start.3 = (bf16[8,3,32,128]{3,2,1,0:T(8,128)(2,1)S(1)}, bf16[8,3,32,128]{3,2,1,0:T(8,128)(2,1)S(1)}, u32[]{:S(2)}, u32[]{:S(2)}) collective-permute-start(bf16[8,3,32,128]{3,2,1,0:T(8,128)(2,1)S(1)} %get-tuple-element.18), channel_id=1, source_target_pairs={{0,2},{1,3},{2,4},{3,5},{4,6},{5,7},{6,0},{7,1},{8,10},{9,11},{10,... | collective-permute-start | bytes 589832 | tf_op jit(solution)/shard_map/ppermute | solution.py:185
  29.3 10.5 %collective-permute-start.4 = (bf16[8,3,32,128]{3,2,1,0:T(8,128)(2,1)S(1)}, bf16[8,3,32,128]{3,2,1,0:T(8,128)(2,1)S(1)}, u32[]{:S(2)}, u32[]{:S(2)}) collective-permute-start(bf16[8,3,32,128]{3,2,1,0:T(8,128)(2,1)S(1)} %get-tuple-element.17), channel_id=1, source_target_pairs={{0,6},{1,7},{2,0},{3,1},{4,2},{5,3},{6,4},{7,5},{8,14},{9,15},{10,... | collective-permute-start | bytes 589832 | tf_op jit(solution)/shard_map/ppermute | solution.py:186
  35.7 7.7 %collective-permute-start.8 = (bf16[8,3,32,128]{3,2,1,0:T(8,128)(2,1)S(1)}, bf16[8,3,32,128]{3,2,1,0:T(8,128)(2,1)S(1)}, u32[]{:S(2)}, u32[]{:S(2)}) collective-permute-start(bf16[8,3,32,128]{3,2,1,0:T(8,128)(2,1)S(1)} %get-tuple-element.14), channel_id=1, source_target_pairs={{0,2},{1,3},{2,4},{3,5},{4,6},{5,7},{6,0},{7,1},{8,10},{9,11},{10,... | collective-permute-start | bytes 589832 | tf_op jit(solution)/shard_map/ppermute | solution.py:185
  37.7 5.8 %collective-permute-start.9 = (bf16[8,3,32,128]{3,2,1,0:T(8,128)(2,1)S(1)}, bf16[8,3,32,128]{3,2,1,0:T(8,128)(2,1)S(1)}, u32[]{:S(2)}, u32[]{:S(2)}) collective-permute-start(bf16[8,3,32,128]{3,2,1,0:T(8,128)(2,1)S(1)} %get-tuple-element.13), channel_id=1, source_target_pairs={{0,6},{1,7},{2,0},{3,1},{4,2},{5,3},{6,4},{7,5},{8,14},{9,15},{10,... | collective-permute-start | bytes 589832 | tf_op jit(solution)/shard_map/ppermute | solution.py:186

commit v5 on v4

--- a/solution.py
+++ b/solution.py
@@ -133,17 +133,24 @@
     )(target, items)
 
 
-def turn_kernel(pieces, out):
+def turn_kernel(pieces, out, turned, sems):
+    copies = []
     for l in range(OWN):
-        out[l] = pieces[:, l].reshape(COLS, LANES).T
+        turned[l] = pieces[:, l].reshape(COLS, LANES).T
+        copies.append(pltpu.make_async_copy(turned.at[l], out.at[l], sems.at[l]))
+        copies[l].start()
+    for copy in copies:
+        copy.wait()
 
 
 def turn_back(pieces):
+    shape = (OWN, LANES, COLS)
     return pl.pallas_call(
         turn_kernel,
         in_specs=[whole_vmem()],
-        out_specs=whole_vmem(),
-        out_shape=jax.ShapeDtypeStruct((OWN, LANES, COLS), jnp.bfloat16),
+        out_specs=pl.BlockSpec(memory_space=pl.ANY),
+        out_shape=jax.ShapeDtypeStruct(shape, jnp.bfloat16),
+        scratch_shapes=[pltpu.VMEM(shape, jnp.bfloat16), pltpu.SemaphoreType.DMA((OWN,))],
         compiler_params=pltpu.CompilerParams(vmem_limit_bytes=VMEM_LIMIT),
         name="turn_back",
     )(pieces)

time: 79.6 us -> 79.5 us (level)
  no operation moved by 1% of the time
where the time goes in v5:
time: 79.5 us; the launch traced here: 79.3 us
  blocking collectives  33.6 us (42%)
  starting transfers between devices  15.2 us (19%)
  Pallas kernels  15 us (19%)
  waiting for transfers between devices  14.5 us (18%)
    all_to_all x2, blocking collectives, exchange(): return lax.all_to_all(x, 'dom', split_axis=0, concat_axis=0, tiled=True)  33.6 us
    pallas_call x2, Pallas kernels, product(): pl.pallas_call(functools.partial(product_kernel, first), grid=(count,), i...  12.2 us
    ppermute x2, waiting for transfers between devices, on_device(): below = lax.ppermute(both(3 * half, 5 * half), 'grp', shift_z(1))  11.1 us
    ppermute x2, starting transfers between devices, on_device(): above = lax.ppermute(both(5 * half, 7 * half), 'grp', shift_z(-1))  4.87 us
    ppermute x2, starting transfers between devices, on_device(): lax.ppermute(both(2 * half, 3 * half, below[half:]), 'grp', shift_z(1))  3.93 us
    ppermute x2, waiting for transfers between devices, on_device(): lax.ppermute(both(2 * half, 3 * half, below[half:]), 'grp', shift_z(1))  3.45 us
    ppermute x2, starting transfers between devices, on_device(): lax.ppermute(both(7 * half, 8 * half, above[:half]), 'grp', shift_z(-1))  3.07 us
    ppermute x2, starting transfers between devices, on_device(): below = lax.ppermute(both(3 * half, 5 * half), 'grp', shift_z(1))  2.75 us
  transfers between devices with their start and end apart: 10, of which 4 were waited for; matrix products, arithmetic and copies ran while one was open for 1% of the time, Pallas kernels for 8%

profile of v5, /device:TPU:0, one launch (start us, length us, event | category | flops | bytes accessed | tf_op | source)
XLA Modules:
  0.0 79.3 jit_solution(9689694677507649759)
XLA Ops:
  0.0 0.0 copy-start
  0.0 6.3 %product.2 = (bf16[4,16,3,32,128]{4,3,2,1,0:T(8,128)(2,1)S(1)}, bf16[4,16,3,32,128]{4,3,2,1,0:T(8,128)(2,1)S(1)}) custom-call(s32[6]{0:T(128)} %bitcast.19, bf16[1,1024,512]{2,1,0:T(8,128)(2,1)} %factor.3, bf16[1,6,1024,1024]{3,2,1,0:T(8,128)(2,1)} %refs_3_.3, bf16[1,6,1024,1024]{3,2,1,0:T(8,128)(2,1)} %refs_3_.3, bf16[1,6,1024,1024]{3,2,1,0:T(8,128)(2,1)} %refs_3_.3, ...), custom_call_target="tpu_custom_call" | custom-call | tf_op jit(solution)/shard_map/product/pallas_call | solution.py:61
  6.3 0.1 collective-permute-start
  6.4 0.0 copy-done
  6.4 5.9 %product.3 = (bf16[4,16,3,32,128]{4,3,2,1,0:T(8,128)(2,1)S(1)}, bf16[4,16,3,32,128]{4,3,2,1,0:T(8,128)(2,1)S(1)}) custom-call(s32[6]{0:T(128)} %bitcast.20, bf16[1,1024,512]{2,1,0:T(8,128)(2,1)S(1)} %copy-done, bf16[1,6,1024,1024]{3,2,1,0:T(8,128)(2,1)} %refs_3_.3, bf16[1,6,1024,1024]{3,2,1,0:T(8,128)(2,1)} %refs_3_.3, bf16[1,6,1024,1024]{3,2,1,0:T(8,128)(2,1)} %refs_3_.3, ...), custom_call_target="tpu_custom_call" | custom-call | tf_op jit(solution)/shard_map/product/pallas_call | solution.py:61
  12.3 0.5 collective-permute-start.5
  12.8 0.0 collective-permute-done.refs_3_
  12.8 0.2 add_convert_fusion.2
  13.0 2.1 %collective-permute-start.1 = (bf16[16,3,32,128]{3,2,1,0:T(8,128)(2,1)S(1)}, bf16[16,3,32,128]{3,2,1,0:T(8,128)(2,1)S(1)}, u32[]{:S(2)}, u32[]{:S(2)}) collective-permute-start(bf16[16,3,32,128]{3,2,1,0:T(8,128)(2,1)S(1)} %get-tuple-element.20), channel_id=1, source_target_pairs={{0,2},{1,3},{2,4},{3,5},{4,6},{5,7},{6,0},{7,1},{8,10},{9,11},{10,... | collective-permute-start | bytes 1179656 | tf_op jit(solution)/shard_map/ppermute | solution.py:190
  15.1 2.2 %collective-permute-start.2 = (bf16[16,3,32,128]{3,2,1,0:T(8,128)(2,1)S(1)}, bf16[16,3,32,128]{3,2,1,0:T(8,128)(2,1)S(1)}, u32[]{:S(2)}, u32[]{:S(2)}) collective-permute-start(bf16[16,3,32,128]{3,2,1,0:T(8,128)(2,1)S(1)} %get-tuple-element.19), channel_id=1, source_target_pairs={{0,6},{1,7},{2,0},{3,1},{4,2},{5,3},{6,4},{7,5},{8,14},{9,15},{10,... | collective-permute-start | bytes 1179656 | tf_op jit(solution)/shard_map/ppermute | solution.py:191
  17.3 0.0 collective-permute-done.5.refs_2_
  17.3 0.2 add_convert_fusion
  17.5 0.6 collective-permute-start.6
  18.2 0.0 copy-start.1
  18.2 0.0 copy-start.2
  18.2 2.7 %collective-permute-start.7 = (bf16[16,3,32,128]{3,2,1,0:T(8,128)(2,1)S(1)}, bf16[16,3,32,128]{3,2,1,0:T(8,128)(2,1)S(1)}, u32[]{:S(2)}, u32[]{:S(2)}) collective-permute-start(bf16[16,3,32,128]{3,2,1,0:T(8,128)(2,1)S(1)} %get-tuple-element.15), channel_id=1, source_target_pairs={{0,6},{1,7},{2,0},{3,1},{4,2},{5,3},{6,4},{7,5},{8,14},{9,15},{10,... | collective-permute-start | bytes 1179656 | tf_op jit(solution)/shard_map/ppermute | solution.py:191
  20.8 6.3 %collective-permute-done.1.refs_4_ = bf16[16,3,32,128]{3,2,1,0:T(8,128)(2,1)S(1)} collective-permute-done((bf16[16,3,32,128]{3,2,1,0:T(8,128)(2,1)S(1)}, bf16[16,3,32,128]{3,2,1,0:T(8,128)(2,1)S(1)}, u32[]{:S(2)}, u32[]{:S(2)}) %collective-permute-start.1) | collective-permute-done | bytes 393248 | tf_op jit(solution)/shard_map/ppermute | solution.py:190
  27.1 0.0 collective-permute-done.2.refs_5_
  27.1 0.2 add_convert_fusion.6
  27.3 2.0 %collective-permute-start.3 = (bf16[8,3,32,128]{3,2,1,0:T(8,128)(2,1)S(1)}, bf16[8,3,32,128]{3,2,1,0:T(8,128)(2,1)S(1)}, u32[]{:S(2)}, u32[]{:S(2)}) collective-permute-start(bf16[8,3,32,128]{3,2,1,0:T(8,128)(2,1)S(1)} %get-tuple-element.18), channel_id=1, source_target_pairs={{0,2},{1,3},{2,4},{3,5},{4,6},{5,7},{6,0},{7,1},{8,10},{9,11},{10,... | collective-permute-start | bytes 589832 | tf_op jit(solution)/shard_map/ppermute | solution.py:192
  29.3 1.5 %collective-permute-start.4 = (bf16[8,3,32,128]{3,2,1,0:T(8,128)(2,1)S(1)}, bf16[8,3,32,128]{3,2,1,0:T(8,128)(2,1)S(1)}, u32[]{:S(2)}, u32[]{:S(2)}) collective-permute-start(bf16[8,3,32,128]{3,2,1,0:T(8,128)(2,1)S(1)} %get-tuple-element.17), channel_id=1, source_target_pairs={{0,6},{1,7},{2,0},{3,1},{4,2},{5,3},{6,4},{7,5},{8,14},{9,15},{10,... | collective-permute-start | bytes 589832 | tf_op jit(solution)/shard_map/ppermute | solution.py:193
  30.8 4.8 %collective-permute-done.6.refs_3_ = bf16[16,3,32,128]{3,2,1,0:T(8,128)(2,1)S(1)} collective-permute-done((bf16[16,3,32,128]{3,2,1,0:T(8,128)(2,1)S(1)}, bf16[16,3,32,128]{3,2,1,0:T(8,128)(2,1)S(1)}, u32[]{:S(2)}, u32[]{:S(2)}) %collective-permute-start.6) | collective-permute-done | bytes 393248 | tf_op jit(solution)/shard_map/ppermute | solution.py:190
  35.6 0.0 collective-permute-done.7.refs_4_
  35.6 0.2 add_convert_fusion.4
  35.7 2.0 %collective-permute-start.8 = (bf16[8,3,32,128]{3,2,1,0:T(8,128)(2,1)S(1)}, bf16[8,3,32,128]{3,2,1,0:T(8,128)(2,1)S(1)}, u32[]{:S(2)}, u32[]{:S(2)}) collective-permute-start(bf16[8,3,32,128]{3,2,1,0:T(8,128)(2,1)S(1)} %get-tuple-element.14), channel_id=1, source_target_pairs={{0,2},{1,3},{2,4},{3,5},{4,6},{5,7},{6,0},{7,1},{8,10},{9,11},{10,... | collective-permute-start | bytes 589832 | tf_op jit(solution)/shard_map/ppermute | solution.py:192
  37.7 1.5 %collective-permute-start.9 = (bf16[8,3,32,128]{3,2,1,0:T(8,128)(2,1)S(1)}, bf16[8,3,32,128]{3,2,1,0:T(8,128)(2,1)S(1)}, u32[]{:S(2)}, u32[]{:S(2)}) collective-permute-start(bf16[8,3,32,128]{3,2,1,0:T(8,128)(2,1)S(1)} %get-tuple-element.13), channel_id=1, source_target_pairs={{0,6},{1,7},{2,0},{3,1},{4,2},{5,3},{6,4},{7,5},{8,14},{9,15},{10,... | collective-permute-start | bytes 589832 | tf_op jit(solution)/shard_map/ppermute | solution.py:193
  39.2 0.5 collective-permute-done.3.refs_6_
  39.8 0.0 collective-permute-done.4.refs_7_
  39.8 0.0 copy-done.1
  39.8 0.0 copy-done.2
  39.8 0.8 finish.2.refs_0_
  40.5 2.9 %collective-permute-done.8.refs_5_ = bf16[8,3,32,128]{3,2,1,0:T(8,128)(2,1)S(1)} collective-permute-done((bf16[8,3,32,128]{3,2,1,0:T(8,128)(2,1)S(1)}, bf16[8,3,32,128]{3,2,1,0:T(8,128)(2,1)S(1)}, u32[]{:S(2)}, u32[]{:S(2)}) %collective-permute-start.8) | collective-permute-done | bytes 196640 | tf_op jit(solution)/shard_map/ppermute | solution.py:192
  43.4 0.0 collective-permute-done.9.refs_6_
  43.5 0.2 finish.3
  43.7 20.0 %all_to_all.10.items = bf16[16,200,128]{2,1,0:T(8,128)(2,1)S(1)} all-to-all(bf16[16,200,128]{2,1,0:T(8,128)(2,1)S(1)} %finish.3), channel_id=1, replica_groups=mesh['dom'=16,'grp'=8] {'dom'}, dimensions={0} | all-to-all | bytes 1638400 | tf_op jit(solution)/shard_map/all_to_all | solution.py:171
  63.7 0.1 reshape.36.target
  63.8 1.0 %sum_blocks.1 = bf16[64,32,128]{2,1,0:T(8,128)(2,1)S(1)} custom-call(s32[96]{0:T(128)S(1)} %reshape.36.target, bf16[16,200,128]{2,1,0:T(8,128)(2,1)S(1)} %all_to_all.10.items), custom_call_target="tpu_custom_call" | custom-call | tf_op jit(solution)/shard_map/sum_blocks/pallas_call | solution.py:125
  64.9 13.5 %all_to_all.11.pieces = bf16[16,4,32,128]{3,2,1,0:T(8,128)(2,1)S(1)} all-to-all(bf16[16,4,32,128]{3,2,1,0:T(8,128)(2,1)S(1)} %bitcast.16), channel_id=1, replica_groups=mesh['dom'=16,'grp'=8] {'dom'}, dimensions={0} | all-to-all | bytes 1048576 | tf_op jit(solution)/shard_map/all_to_all | solution.py:171
  78.4 0.9 %turn_back.1 = bf16[4,128,512]{2,1,0:T(8,128)(2,1)} custom-call(bf16[16,4,32,128]{3,2,1,0:T(8,128)(2,1)S(1)} %all_to_all.11.pieces), custom_call_target="tpu_custom_call" | custom-call | tf_op jit(solution)/shard_map/turn_back/pallas_call | solution.py:148
  (1 shorter events, 0.0 us)
Async XLA Ops:
  0.0 6.4 %copy-start = (bf16[1,1024,512]{2,1,0:T(8,128)(2,1)S(1)}, bf16[1,1024,512]{2,1,0:T(8,128)(2,1)}, u32[]{:S(2)}) copy-start(bf16[1,1024,512]{2,1,0:T(8,128)(2,1)} %factor.3) | copy-start | bytes 3145732
  6.3 6.5 %collective-permute-start = (bf16[4,16,3,32,128]{4,3,2,1,0:T(8,128)(2,1)S(1)}, bf16[4,16,3,32,128]{4,3,2,1,0:T(8,128)(2,1)S(1)}, u32[]{:S(2)}, u32[]{:S(2)}) collective-permute-start(bf16[4,16,3,32,128]{4,3,2,1,0:T(8,128)(2,1)S(1)} %get-tuple-element.10), channel_id=1, source_target_pairs={{0,1},{1,0},{2,3},{3,2},{4,5},{5,4},{6,7},{7,6},{8,9},{9,8},{10,11... | collective-permute-start | bytes 4718600 | tf_op jit(solution)/shard_map/ppermute | solution.py:183
  12.3 5.0 %collective-permute-start.5 = (bf16[4,16,3,32,128]{4,3,2,1,0:T(8,128)(2,1)S(1)}, bf16[4,16,3,32,128]{4,3,2,1,0:T(8,128)(2,1)S(1)}, u32[]{:S(2)}, u32[]{:S(2)}) collective-permute-start(bf16[4,16,3,32,128]{4,3,2,1,0:T(8,128)(2,1)S(1)} %get-tuple-element.12), channel_id=1, source_target_pairs={{0,1},{1,0},{2,3},{3,2},{4,5},{5,4},{6,7},{7,6},{8,9},{9,8},{10,11... | collective-permute-start | bytes 4718600 | tf_op jit(solution)/shard_map/ppermute | solution.py:183
  13.0 14.1 %collective-permute-start.1 = (bf16[16,3,32,128]{3,2,1,0:T(8,128)(2,1)S(1)}, bf16[16,3,32,128]{3,2,1,0:T(8,128)(2,1)S(1)}, u32[]{:S(2)}, u32[]{:S(2)}) collective-permute-start(bf16[16,3,32,128]{3,2,1,0:T(8,128)(2,1)S(1)} %get-tuple-element.20), channel_id=1, source_target_pairs={{0,2},{1,3},{2,4},{3,5},{4,6},{5,7},{6,0},{7,1},{8,10},{9,11},{10,... | collective-permute-start | bytes 1179656 | tf_op jit(solution)/shard_map/ppermute | solution.py:190
  15.1 12.0 %collective-permute-start.2 = (bf16[16,3,32,128]{3,2,1,0:T(8,128)(2,1)S(1)}, bf16[16,3,32,128]{3,2,1,0:T(8,128)(2,1)S(1)}, u32[]{:S(2)}, u32[]{:S(2)}) collective-permute-start(bf16[16,3,32,128]{3,2,1,0:T(8,128)(2,1)S(1)} %get-tuple-element.19), channel_id=1, source_target_pairs={{0,6},{1,7},{2,0},{3,1},{4,2},{5,3},{6,4},{7,5},{8,14},{9,15},{10,... | collective-permute-start | bytes 1179656 | tf_op jit(solution)/shard_map/ppermute | solution.py:191
  17.5 18.0 %collective-permute-start.6 = (bf16[16,3,32,128]{3,2,1,0:T(8,128)(2,1)S(1)}, bf16[16,3,32,128]{3,2,1,0:T(8,128)(2,1)S(1)}, u32[]{:S(2)}, u32[]{:S(2)}) collective-permute-start(bf16[16,3,32,128]{3,2,1,0:T(8,128)(2,1)S(1)} %get-tuple-element.16), channel_id=1, source_target_pairs={{0,2},{1,3},{2,4},{3,5},{4,6},{5,7},{6,0},{7,1},{8,10},{9,11},{10,... | collective-permute-start | bytes 1179656 | tf_op jit(solution)/shard_map/ppermute | solution.py:190
  18.2 21.6 %copy-start.1 = (s32[1,6,1]{1,2,0:T(1,128)S(1)}, s32[1,6,1]{1,2,0:T(1,128)}, u32[]{:S(2)}) copy-start(s32[1,6,1]{1,2,0:T(1,128)} %param.8) | copy-start | bytes 76
  18.2 21.6 %copy-start.2 = (s32[1,6]{1,0:T(1,128)S(1)}, s32[1,6]{1,0:T(1,128)}, u32[]{:S(2)}) copy-start(s32[1,6]{1,0:T(1,128)} %param.9) | copy-start | bytes 76
  18.2 17.4 %collective-permute-start.7 = (bf16[16,3,32,128]{3,2,1,0:T(8,128)(2,1)S(1)}, bf16[16,3,32,128]{3,2,1,0:T(8,128)(2,1)S(1)}, u32[]{:S(2)}, u32[]{:S(2)}) collective-permute-start(bf16[16,3,32,128]{3,2,1,0:T(8,128)(2,1)S(1)} %get-tuple-element.15), channel_id=1, source_target_pairs={{0,6},{1,7},{2,0},{3,1},{4,2},{5,3},{6,4},{7,5},{8,14},{9,15},{10,... | collective-permute-start | bytes 1179656 | tf_op jit(solution)/shard_map/ppermute | solution.py:191
  27.3 12.5 %collective-permute-start.3 = (bf16[8,3,32,128]{3,2,1,0:T(8,128)(2,1)S(1)}, bf16[8,3,32,128]{3,2,1,0:T(8,128)(2,1)S(1)}, u32[]{:S(2)}, u32[]{:S(2)}) collective-permute-start(bf16[8,3,32,128]{3,2,1,0:T(8,128)(2,1)S(1)} %get-tuple-element.18), channel_id=1, source_target_pairs={{0,2},{1,3},{2,4},{3,5},{4,6},{5,7},{6,0},{7,1},{8,10},{9,11},{10,... | collective-permute-start | bytes 589832 | tf_op jit(solution)/shard_map/ppermute | solution.py:192
  29.3 10.5 %collective-permute-start.4 = (bf16[8,3,32,128]{3,2,1,0:T(8,128)(2,1)S(1)}, bf16[8,3,32,128]{3,2,1,0:T(8,128)(2,1)S(1)}, u32[]{:S(2)}, u32[]{:S(2)}) collective-permute-start(bf16[8,3,32,128]{3,2,1,0:T(8,128)(2,1)S(1)} %get-tuple-element.17), channel_id=1, source_target_pairs={{0,6},{1,7},{2,0},{3,1},{4,2},{5,3},{6,4},{7,5},{8,14},{9,15},{10,... | collective-permute-start | bytes 589832 | tf_op jit(solution)/shard_map/ppermute | solution.py:193
  35.7 7.7 %collective-permute-start.8 = (bf16[8,3,32,128]{3,2,1,0:T(8,128)(2,1)S(1)}, bf16[8,3,32,128]{3,2,1,0:T(8,128)(2,1)S(1)}, u32[]{:S(2)}, u32[]{:S(2)}) collective-permute-start(bf16[8,3,32,128]{3,2,1,0:T(8,128)(2,1)S(1)} %get-tuple-element.14), channel_id=1, source_target_pairs={{0,2},{1,3},{2,4},{3,5},{4,6},{5,7},{6,0},{7,1},{8,10},{9,11},{10,... | collective-permute-start | bytes 589832 | tf_op jit(solution)/shard_map/ppermute | solution.py:192
  37.7 5.8 %collective-permute-start.9 = (bf16[8,3,32,128]{3,2,1,0:T(8,128)(2,1)S(1)}, bf16[8,3,32,128]{3,2,1,0:T(8,128)(2,1)S(1)}, u32[]{:S(2)}, u32[]{:S(2)}) collective-permute-start(bf16[8,3,32,128]{3,2,1,0:T(8,128)(2,1)S(1)} %get-tuple-element.13), channel_id=1, source_target_pairs={{0,6},{1,7},{2,0},{3,1},{4,2},{5,3},{6,4},{7,5},{8,14},{9,15},{10,... | collective-permute-start | bytes 589832 | tf_op jit(solution)/shard_map/ppermute | solution.py:193
